TPU v7x, 32 devices: a whole 2x2x4 slice. The times are simulated.
32 devices in a mesh: bx: 8 (over y, x, core), by: 4 (over z).
Axes of the slice: x: 2, y: 2, z: 4, core: 2. Of those that a mesh axis runs over, the one named last changes fastest.
Arguments:
- interface_velocity: float32 [3, 2048, 2048], P(None, 'bx', 'by'), may hold values from -6 to 6
- history: float32 [6, 2, 3, 256, 8, 4, 512], P(None, None, None, 'by', 'bx'), may hold values from -6 to 6
- kernel: float32 [7, 256, 8, 4, 512], P(None, 'by', 'bx'), may hold values from -6 to 6
- velocity: float32 [3, 4, 2048, 2048], P(None, None, 'bx', 'by'), may hold values from -6 to 6
- stress: float32 [6, 4, 2048, 2048], P(None, None, 'bx', 'by'), may hold values from -6 to 6
- cohesion: float32 [4, 2048, 2048], P(None, 'bx', 'by'), may hold values from 0.5 to 4
Outputs:
- velocity_new: float32 [3, 4, 2048, 2048], P(None, None, 'bx', 'by')
- stress_new: float32 [6, 4, 2048, 2048], P(None, None, 'bx', 'by')
All inputs are finite; a program needn't handle non-finite values.
Results may differ from a plain program's by a relative error of at most 0.00005.
Values sent between devices are 32-bit elements; how exact they have to be, the bound alone decides.
A program may use at most 192 MiB of HBM per device.

v0:
```python
from functools import partial
import math

import jax
import jax.numpy as jnp
import numpy as np
from jax import lax
from jax.experimental import pallas as pl
from jax.experimental.pallas import tpu as pltpu
from jax.sharding import PartitionSpec as P

COURANT = 0.3
FRICTION = 0.6
F32 = jnp.float32
BF16 = jnp.bfloat16


def halves(table):
    high = np.asarray(table, np.float32).astype(BF16)
    low = (np.asarray(table, np.float64) - high.astype(np.float64)).astype(BF16)
    return np.stack([high, low])


def square_table(length):
    index = np.arange(length)
    angle = 2.0 * math.pi / length * (index[:, None] * index[None, :] % length)
    return jnp.asarray(np.stack([halves(np.cos(angle)), halves(np.sin(angle))]))


def split(value):
    high = value.astype(BF16)
    return high, (value - high.astype(F32)).astype(BF16)


def product(value, table, left):
    def dot(a, b):
        if left:
            a, b = b, a
        return lax.dot_general(a, b, (((1,), (0,)), ((), ())), preferred_element_type=F32)

    return dot(value[0], table[0]) + (dot(value[0], table[1]) + dot(value[1], table[0]))


def complex_product(real_part, imag_part, table_ref, sign, left):
    cos = (table_ref[0, 0], table_ref[0, 1])
    sin = (table_ref[1, 0], table_ref[1, 1])
    real_part, imag_part = split(real_part), split(imag_part)
    return (
        product(real_part, cos, left) - sign * product(imag_part, sin, left),
        product(imag_part, cos, left) + sign * product(real_part, sin, left),
    )


def root(index, count):
    angle = 2.0 * math.pi * (index % count) / count
    cos, sin = math.cos(angle), math.sin(angle)
    return [float(round(v)) if abs(v - round(v)) < 1e-12 else v for v in (cos, sin)]


def add_term(total, factor, value):
    if factor == 0.0:
        return total
    term = value if factor == 1.0 else (-value if factor == -1.0 else factor * value)
    return term if total is None else total + term


def strike_forward(count, x_ref, o_ref):
    for r in range(count):
        real_part = imag_part = None
        for b in range(count):
            cos, sin = root(r * b, count)
            real_part = add_term(real_part, cos, x_ref[b])
            imag_part = add_term(imag_part, -sin, x_ref[b])
        o_ref[r, 0] = real_part
        o_ref[r, 1] = jnp.zeros_like(real_part) if imag_part is None else imag_part


def strike_inverse(count, scale, x_ref, o_ref):
    for b in range(count):
        total = None
        for r in range(count):
            cos, sin = root(r * b, count)
            total = add_term(total, cos, x_ref[r, 0])
            total = add_term(total, -sin, x_ref[r, 1])
        o_ref[b] = scale * total


def strike_cells_dft(sign, x_ref, tw_ref, table_ref, o_ref, held):
    blocks, _, rows, _ = x_ref.shape
    for s in range(blocks):
        for z in range(2):
            held[z, pl.ds(s * rows, rows), :] = x_ref[s, z]
    cos, sin = tw_ref[:, 0:1], sign * tw_ref[:, 1:2]
    real_part, imag_part = held[0], held[1]
    if sign < 0:
        real_part, imag_part = (
            real_part * cos - imag_part * sin,
            real_part * sin + imag_part * cos,
        )
    real_part, imag_part = complex_product(real_part, imag_part, table_ref, sign, True)
    if sign > 0:
        real_part, imag_part = (
            real_part * cos - imag_part * sin,
            real_part * sin + imag_part * cos,
        )
    held[0] = real_part
    held[1] = imag_part
    blocks, _, rows, _ = o_ref.shape
    for s in range(blocks):
        for z in range(2):
            o_ref[s, z] = held[z, pl.ds(s * rows, rows), :]


def dip_response(scale, x_refs, tw_ref, table_ref, now_ref, past_ref, o_refs, held):
    count, _, rows, width = x_refs[0].shape
    for h, x_ref in enumerate(x_refs):
        part = slice(h * width, (h + 1) * width)
        for l in range(count):
            real_part = imag_part = None
            for j in range(count):
                cos, sin = root(l * j, count)
                real_part = add_term(real_part, cos, x_ref[j, 0])
                real_part = add_term(real_part, sin, x_ref[j, 1])
                imag_part = add_term(imag_part, cos, x_ref[j, 1])
                imag_part = add_term(imag_part, -sin, x_ref[j, 0])
            cos, sin = tw_ref[0, l : l + 1, part], tw_ref[1, l : l + 1, part]
            held[0, pl.ds(l * rows, rows), part] = real_part * cos + imag_part * sin
            held[1, pl.ds(l * rows, rows), part] = imag_part * cos - real_part * sin
    real_part, imag_part = complex_product(held[0], held[1], table_ref, -1.0, False)
    weight = scale * now_ref[...]
    real_part = weight * real_part + past_ref[0]
    imag_part = weight * imag_part + past_ref[1]
    real_part, imag_part = complex_product(real_part, imag_part, table_ref, 1.0, False)
    held[0] = real_part
    held[1] = imag_part
    for l in range(count):
        cos, sin = tw_ref[0, l : l + 1, :], tw_ref[1, l : l + 1, :]
        real_part = held[0, pl.ds(l * rows, rows), :]
        imag_part = held[1, pl.ds(l * rows, rows), :]
        held[0, pl.ds(l * rows, rows), :] = real_part * cos - imag_part * sin
        held[1, pl.ds(l * rows, rows), :] = imag_part * cos + real_part * sin
    for h, o_ref in enumerate(o_refs):
        part = slice(h * width, (h + 1) * width)
        for j in range(count):
            real_part = imag_part = None
            for l in range(count):
                cos, sin = root(l * j, count)
                lr = held[0, pl.ds(l * rows, rows), part]
                li = held[1, pl.ds(l * rows, rows), part]
                real_part = add_term(real_part, cos, lr)
                real_part = add_term(real_part, -sin, li)
                imag_part = add_term(imag_part, cos, li)
                imag_part = add_term(imag_part, sin, lr)
            o_ref[j, 0] = real_part
            o_ref[j, 1] = imag_part


def rows_diff(value, before, after):
    count = value.shape[0]
    row = lax.broadcasted_iota(jnp.int32, value.shape, 0)
    low = jnp.where(row == 0, before, pltpu.roll(value, 1, 0))
    high = jnp.where(row == count - 1, after, pltpu.roll(value, count - 1, 0))
    return 0.5 * (high - low)


def cols_diff(value, before, after):
    count = value.shape[1]
    col = lax.broadcasted_iota(jnp.int32, value.shape, 1)
    low = jnp.where(col == 0, before, pltpu.roll(value, 1, 1))
    high = jnp.where(col == count - 1, after, pltpu.roll(value, count - 1, 1))
    return 0.5 * (high - low)


def strike_edges(low_ref, prev_ref, high_ref, next_ref, slot, component, z):
    i, last = pl.program_id(0), pl.num_programs(0) - 1
    before = jnp.where(i == 0, low_ref[slot, z : z + 1, :], prev_ref[component, z, 7:8, :])
    after = jnp.where(i == last, high_ref[slot, z : z + 1, :], next_ref[component, z, 0:1, :])
    return before, after


def velocity_step(s_ref, prev_ref, next_ref, low_ref, high_ref, col_ref, v_ref, t_ref, o_ref, c_ref, l_ref, h_ref):
    layers = v_ref.shape[1]
    width = v_ref.shape[3]
    half = 3 * layers
    for component, (sx, sy, sz) in enumerate(((0, 3, 4), (3, 1, 5), (4, 5, 2))):
        for z in range(layers):
            before, after = strike_edges(low_ref, prev_ref, high_ref, next_ref, component, sx, z)
            total = rows_diff(s_ref[sx, z], before, after)
            k = component * layers + z
            total = total + cols_diff(
                s_ref[sy, z], col_ref[:, k : k + 1], col_ref[:, half + k : half + k + 1]
            )
            low = t_ref[component] if z == 0 else s_ref[sz, z - 1]
            if z + 1 < layers:
                total = total + 0.5 * (s_ref[sz, z + 1] - low)
            else:
                total = total - 0.5 * low
            value = v_ref[component, z] + COURANT * total
            o_ref[component, z] = value
            c_ref[:, k : k + 1] = value[:, 0:1]
            c_ref[:, half + k : half + k + 1] = value[:, width - 1 : width]

            @pl.when(pl.program_id(0) == 0)
            def _():
                l_ref[component, z : z + 1, :] = value[0:1, :]

            @pl.when(pl.program_id(0) == pl.num_programs(0) - 1)
            def _():
                h_ref[component, z : z + 1, :] = value[-1:, :]


def stress_step(v_ref, prev_ref, next_ref, low_ref, high_ref, col_ref, w_ref, s_ref, y_ref, o_ref):
    layers = v_ref.shape[1]
    half = 3 * layers
    for z in range(layers):
        dx, dy, dz = [], [], []
        for c in range(3):
            before, after = strike_edges(low_ref, prev_ref, high_ref, next_ref, c, c, z)
            k = c * layers + z
            dx.append(rows_diff(v_ref[c, z], before, after))
            dy.append(
                cols_diff(v_ref[c, z], col_ref[:, k : k + 1], col_ref[:, half + k : half + k + 1])
            )
            low = w_ref[c] if z == 0 else v_ref[c, z - 1]
            if z + 1 < layers:
                dz.append(0.5 * (v_ref[c, z + 1] - low))
            else:
                dz.append(-0.5 * low)
        dilation = dx[0] + dy[1] + dz[2]
        xx = s_ref[0, z] + COURANT * (dilation + 2.0 * dx[0])
        yy = s_ref[1, z] + COURANT * (dilation + 2.0 * dy[1])
        zz = s_ref[2, z] + COURANT * (dilation + 2.0 * dz[2])
        xy = s_ref[3, z] + COURANT * (dy[0] + dx[1])
        xz = s_ref[4, z] + COURANT * (dz[0] + dx[2])
        yz = s_ref[5, z] + COURANT * (dz[1] + dy[2])
        pressure = (xx + yy + zz) / 3.0
        xx, yy, zz = xx - pressure, yy - pressure, zz - pressure
        shear = jnp.sqrt(0.5 * (xx * xx + yy * yy + zz * zz) + (xy * xy + xz * xz + yz * yz))
        limit = y_ref[z] + FRICTION * jnp.maximum(-pressure, 0.0)
        factor = limit / jnp.maximum(shear, limit)
        o_ref[0, z] = pressure + factor * xx
        o_ref[1, z] = pressure + factor * yy
        o_ref[2, z] = pressure + factor * zz
        o_ref[3, z] = factor * xy
        o_ref[4, z] = factor * xz
        o_ref[5, z] = factor * yz


def whole_block(shape):
    return pl.BlockSpec(shape, lambda *_: (0,) * len(shape))


def struct(shape):
    return jax.ShapeDtypeStruct(shape, F32)


def cost(flops, *arrays):
    moved = sum(math.prod(a.shape) * a.dtype.itemsize for a in arrays)
    return pl.CostEstimate(flops=int(flops), bytes_accessed=int(moved), transcendentals=0)


def ring(axis):
    count = lax.axis_size(axis)
    forward = [(i, (i + 1) % count) for i in range(count)]
    return forward, [(b, a) for a, b in forward]


def edges(first, last, axis):
    forward, backward = ring(axis)
    return lax.ppermute(last, axis, forward), lax.ppermute(first, axis, backward)


def fault_kernel(
    scale,
    face_ref,
    strike_tw_ref,
    strike_table_ref,
    dip_tw_ref,
    dip_table_ref,
    now_ref,
    past_ref,
    o_ref,
    x1,
    b1,
    b2,
    t1,
    t2,
    u1,
    u2,
    w1,
    w2,
    y1,
    held,
    held_part,
    send_sem,
    recv_sem,
):
    count, narrow = x1.shape[0], x1.shape[-1]
    parts = count // past_ref.shape[0]
    sizes = {"bx": lax.axis_size("bx"), "by": lax.axis_size("by")}
    place = {"bx": lax.axis_index("bx"), "by": lax.axis_index("by")}

    def device(axis, target):
        if axis == "bx":
            return (target, place["by"])
        return (place["bx"], target)

    barrier = pltpu.get_barrier_semaphore()
    for axis in ("bx", "by"):

        @pl.loop(1, sizes[axis])
        def _(k):
            target = lax.rem(place[axis] + k, sizes[axis])
            pl.semaphore_signal(
                barrier, 1, device_id=device(axis, target), device_id_type=pl.DeviceIdType.MESH
            )

    pl.semaphore_wait(barrier, sizes["bx"] + sizes["by"] - 2)

    def piece(ref, g, slot):
        if len(ref.shape) == 4 and ref.shape[0] != count:
            return ref.at[g // parts, slot, :, pl.ds(pl.multiple_of(g % parts * narrow, narrow), narrow)]
        if ref is face_ref or ref is o_ref:
            return ref.at[g, slot, :, pl.ds(0, narrow)]
        return ref.at[g, slot]

    def copy(stage, axis, c, k, source, landing):
        me = place[axis]
        target = lax.rem(me + k, sizes[axis])
        return pltpu.make_async_remote_copy(
            src_ref=piece(source, c, target),
            dst_ref=piece(landing, c, me),
            send_sem=send_sem.at[stage, c, k],
            recv_sem=recv_sem.at[stage, c, k],
            device_id=device(axis, target),
            device_id_type=pl.DeviceIdType.MESH,
        )

    def own(stage, axis, c, source, landing):
        me = place[axis]
        return pltpu.make_async_copy(
            piece(source, c, me), piece(landing, c, me), recv_sem.at[stage, c, 0]
        )

    def send(stage, axis, c, source, landing):
        @pl.loop(1, sizes[axis])
        def _(k):
            copy(stage, axis, c, k, source, landing).start()

        own(stage, axis, c, source, landing).start()

    def receive(stage, axis, c, source, landing):
        own(stage, axis, c, source, landing).wait()

        @pl.loop(1, sizes[axis])
        def _(k):
            copy(stage, axis, c, k, source, landing).wait()

    stages = (
        ("bx", face_ref, x1),
        ("bx", b1, b2),
        ("by", t1, t2),
        ("by", u1, u2),
        ("bx", w1, w2),
        ("bx", y1, o_ref),
    )

    def go(stage, g):
        axis, source, landing = stages[stage]
        send(stage, axis, g, source, landing)

    def take(stage, g):
        axis, source, landing = stages[stage]
        receive(stage, axis, g, source, landing)

    def enter(g):
        take(0, g)
        strike_forward(sizes["bx"], x1.at[g], b1.at[g])
        go(1, g)

    def across(g):
        take(1, g)
        strike_cells_dft(-1.0, b2.at[g], strike_tw_ref, strike_table_ref, t1.at[g], held_part)
        go(2, g)

    def back(g):
        take(3, g)
        strike_cells_dft(1.0, u2.at[g], strike_tw_ref, strike_table_ref, w1.at[g], held_part)
        go(4, g)

    def leave(g):
        take(4, g)
        strike_inverse(sizes["bx"], scale, w2.at[g], y1.at[g])
        go(5, g)

    go(0, 0)
    go(0, 1)

    @pl.loop(0, count + 1)
    def _(g):
        @pl.when(g < count)
        def _():
            enter(g)

        @pl.when(g + 2 < count)
        def _():
            go(0, g + 2)

        @pl.when(g > 0)
        def _():
            across(g - 1)

    @pl.loop(0, past_ref.shape[0])
    def _(c):
        for h in range(parts):
            take(2, c * parts + h)
        dip_response(
            scale,
            [t2.at[c * parts + h] for h in range(parts)],
            dip_tw_ref,
            dip_table_ref,
            now_ref,
            past_ref.at[c],
            [u1.at[c * parts + h] for h in range(parts)],
            held,
        )
        for h in range(parts):
            go(3, c * parts + h)

    @pl.loop(0, count + 1)
    def _(g):
        @pl.when(g < count)
        def _():
            back(g)

        @pl.when(g > 0)
        def _():
            leave(g - 1)

    @pl.loop(0, count)
    def _(g):
        take(5, g)


def fault_traction(interface, now, past, tables, scale):
    strike_count, dip_count = lax.axis_size("bx"), lax.axis_size("by")
    count, cells, width = interface.shape
    rows, modes = cells // strike_count, cells // dip_count
    parts = 2 if width % 256 == 0 else 1
    narrow = width // parts
    face = interface.reshape(count, strike_count, rows, width)
    chunks = count * parts
    flat = (chunks, strike_count, rows, narrow)
    wide = (chunks, strike_count, 2, rows, narrow)
    tall = (chunks, dip_count, 2, modes, narrow)
    peers = max(strike_count, dip_count)
    operands = (face, *tables, now, past)
    out = pl.pallas_call(
        partial(fault_kernel, scale),
        out_shape=struct(face.shape),
        in_specs=[pl.BlockSpec(memory_space=pltpu.VMEM)] * len(operands),
        out_specs=pl.BlockSpec(memory_space=pltpu.VMEM),
        scratch_shapes=[
            *[pltpu.VMEM(s, F32) for s in (flat, wide, wide, tall, tall, tall, tall, wide, wide)],
            pltpu.VMEM(flat, F32),
            pltpu.VMEM((2, cells, width), F32),
            pltpu.VMEM((2, cells, narrow), F32),
            pltpu.SemaphoreType.DMA((6, chunks, peers)),
            pltpu.SemaphoreType.DMA((6, chunks, peers)),
        ],
        compiler_params=pltpu.CompilerParams(
            collective_id=0, has_side_effects=True, vmem_limit_bytes=60 * 1024 * 1024
        ),
        name="fault_traction",
    )(*operands)
    return out.reshape(count, cells, width)


def tile_spec(shape, tile):
    block = shape[:-2] + (tile, shape[-1])
    lead = (0,) * (len(shape) - 2)
    return pl.BlockSpec(block, lambda i: lead + (i, 0))


def halo_specs(shape, tile):
    block = shape[:-2] + (8, shape[-1])
    lead = (0,) * (len(shape) - 2)
    step, last = tile // 8, shape[-2] // 8 - 1
    return [
        pl.BlockSpec(block, lambda i: lead + (jnp.maximum(i * step - 1, 0), 0)),
        pl.BlockSpec(block, lambda i: lead + (jnp.minimum((i + 1) * step, last), 0)),
    ]


def local(interface_velocity, history, kernel, velocity, stress, cohesion):
    strike_count, dip_count = lax.axis_size("bx"), lax.axis_size("by")
    _, layers, cells, width = velocity.shape
    strike_length, dip_length = cells * strike_count, width * dip_count
    scale = 1.0 / math.sqrt(strike_length * dip_length)
    angle = (2.0 * math.pi / strike_length) * (
        jnp.arange(cells, dtype=jnp.int32) * lax.axis_index("bx")
    ).astype(F32)
    strike_tw = jnp.stack([jnp.cos(angle), jnp.sin(angle)], axis=1)
    lane = np.outer(np.arange(dip_count), np.arange(width)) * (2.0 * math.pi / dip_length)
    dip_tw = jnp.asarray(np.stack([np.cos(lane), np.sin(lane)]).astype(np.float32))
    dip_table = lax.optimization_barrier(square_table(width))
    if width % cells == 0:
        strike_table = dip_table[:, :, :: width // cells, :cells]
    else:
        strike_table = square_table(cells)
    tables = (strike_tw, strike_table, dip_tw, dip_table)

    past = kernel[1] * history[0]
    for h in range(1, history.shape[0]):
        past = past + kernel[h + 1] * history[h]
    modes = history.shape[3]
    past = past.reshape(2, 3, modes, dip_count, width).transpose(1, 0, 3, 2, 4)
    past = past.reshape(3, 2, cells, width)
    now = kernel[0].reshape(modes, dip_count, width).transpose(1, 0, 2).reshape(cells, width)

    traction = fault_traction(interface_velocity, now, past, tables, scale)

    tile = min(32, cells)
    grid = (cells // tile,)
    col_shape = (cells, 6 * layers)

    def columns(first, last):
        low, high = edges(first, last, "by")
        return jnp.concatenate([low, high], axis=1)

    def side(position):
        flat = [stress[c, :, :, position] for c in (3, 1, 5)]
        return jnp.concatenate(flat, axis=0).T

    def line(position):
        return jnp.stack([stress[c, :, position, :] for c in (0, 3, 4)])

    cols = columns(side(0), side(width - 1))
    low, high = edges(line(0), line(cells - 1), "bx")
    velocity_new, new_cols, first, last = pl.pallas_call(
        velocity_step,
        grid=grid,
        in_specs=[
            tile_spec(stress.shape, tile),
            *halo_specs(stress.shape, tile),
            whole_block(low.shape),
            whole_block(high.shape),
            tile_spec(col_shape, tile),
            tile_spec(velocity.shape, tile),
            tile_spec(traction.shape, tile),
        ],
        out_specs=[
            tile_spec(velocity.shape, tile),
            tile_spec(col_shape, tile),
            whole_block(low.shape),
            whole_block(low.shape),
        ],
        out_shape=[struct(velocity.shape), struct(col_shape), struct(low.shape), struct(low.shape)],
        cost_estimate=cost(1e7, stress, velocity, velocity),
        name="velocity_step",
    )(stress, stress, stress, low, high, cols, velocity, traction)
    half = 3 * layers
    cols = columns(new_cols[:, :half], new_cols[:, half:])
    low, high = edges(first, last, "bx")
    stress_new = pl.pallas_call(
        stress_step,
        grid=grid,
        in_specs=[
            tile_spec(velocity.shape, tile),
            *halo_specs(velocity.shape, tile),
            whole_block(low.shape),
            whole_block(high.shape),
            tile_spec(col_shape, tile),
            tile_spec(interface_velocity.shape, tile),
            tile_spec(stress.shape, tile),
            tile_spec(cohesion.shape, tile),
        ],
        out_specs=tile_spec(stress.shape, tile),
        out_shape=struct(stress.shape),
        cost_estimate=cost(2e7, stress, stress, velocity),
        name="stress_step",
    )(velocity_new, velocity_new, velocity_new, low, high, cols, interface_velocity, stress, cohesion)
    return velocity_new, stress_new


def solution(mesh):
    return jax.shard_map(
        local,
        mesh=mesh,
        in_specs=(
            P(None, "bx", "by"),
            P(None, None, None, "by", "bx", None, None),
            P(None, "by", "bx", None, None),
            P(None, None, "bx", "by"),
            P(None, None, "bx", "by"),
            P(None, "bx", "by"),
        ),
        out_specs=(P(None, None, "bx", "by"), P(None, None, "bx", "by")),
        check_vma=False,
    )
```

profile of v0, /device:TPU:0, one launch (start us, length us, event | category | flops | bytes accessed | tf_op | source)
XLA Modules:
  0.0 275.8 jit_solution(10951714385067809872)
XLA Ops:
  0.6 1.0 fusion.14
  1.7 0.5 collective-permute-start
  2.3 2.9 %collective-permute-start.1 = (f32[3,4,512]{2,1,0:T(4,128)S(1)}, f32[3,4,512]{2,1,0:T(4,128)S(1)}, u32[]{:S(2)}, u32[]{:S(2)}) collective-permute-start(f32[3,4,512]{2,1,0:T(4,128)S(1)} %pad_maximum_fusion.2), channel_id=1, source_target_pairs={{4,0},{8,4},{12,8},{16,12},{20,16},{24,20},{28,24},{0,28},{5,1},{9... | collective-permute-start | bytes 73736 | tf_op jit(solution)/shard_map/ppermute | solution.py:270
  5.2 2.4 fusion.13
  8.3 4.4 %collective-permute-start.3 = (f32[256,12]{0,1:T(8,128)S(1)}, f32[256,12]{0,1:T(8,128)S(1)}, u32[]{:S(2)}, u32[]{:S(2)}) collective-permute-start(f32[256,12]{0,1:T(8,128)S(1)} %maximum_bitcast_fusion.1), channel_id=1, source_target_pairs={{1,0},{2,1},{3,2},{0,3},{5,4},{6,5},{7,6},{4,7},{9,8},{10,9},{11,1... | collective-permute-start | bytes 36872 | tf_op jit(solution)/shard_map/ppermute | solution.py:270
  13.4 3.6 %slice_bitcast_fusion.10 = (f32[64,4,512]{2,1,0:T(4,128)S(1)}, f32[64,4,512]{2,1,0:T(4,128)S(1)}, f32[64,4,512]{2,1,0:T(4,128)S(1)}, f32[64,4,512]{2,1,0:T(4,128...) fusion(f32[7,64,1,4,512]{4,3,2,1,0:T(4,128)} %param.10), kind=kLoop, calls=%fused_computation.22 | loop fusion | bytes 7340032 | tf_op jit(solution)/shard_map/mul | solution.py:513
  17.0 7.9 %fusion.2 = f32[3,2,4,64,512]{4,2,3,0,1:T(4,128)S(1)} fusion(f32[6,2,3,64,1,4,512]{6,5,3,2,1,4,0:T(4,128)} %bitcast.91, f32[6,2,3,64,1,4,512]{6,5,4,3,2,1,0:T(4,128)} %param.9, f32[64,4,512]{2,1,0:T(4,128)S(1)} %get-tuple-element.27, f32[64,4,512]{2,1,0:T(4,128)S(1)} %get-tuple-element.28, f32[64,4,512]{2,1,0:T(4,128)S(1)} %get-tuple-element.23, ...), kind=kLoop, calls=%fused_computation.3 | loop fusion | flops 8650752 | bytes 25165824 | tf_op jit(solution)/shard_map/transpose | solution.py:517
  24.9 0.8 copy.72.strike_tw_ref
  25.7 7.1 %slice.96.strike_table_ref = bf16[2,2,256,256]{3,2,1,0:T(8,128)(2,1)} slice(bf16[2,2,512,512]{3,2,1,0:T(8,128)(2,1)} %constant.13.clone.dip_table_ref), slice={[0:2:1], [0:2:1], [0:512:2], [0:256:1]} | slice | bytes 1048576 | tf_op jit(solution)/shard_map/slice | solution.py:508
  32.9 2.6 copy.71
  35.5 1.0 copy.65
  36.5 182.5 %fault_traction.1 = f32[3,8,32,512]{3,2,1,0:T(8,128)} custom-call(f32[3,8,32,512]{3,2,1,0:T(8,128)} %bitcast.93, f32[256,2]{1,0:T(8,128)} %copy.72.strike_tw_ref, bf16[2,2,256,256]{3,2,1,0:T(8,128)(2,1)} %slice.96.strike_table_ref, f32[2,4,512]{2,1,0:T(4,128)} %constant.12.clone.dip_tw_ref, bf16[2,2,512,512]{3,2,1,0:T(8,128)(2,1)} %constant.13.clone.dip_table_ref, ...), custom_call_target="tpu_custom_call" | custom-call | tf_op jit(solution)/shard_map/fault_traction/pallas_call | solution.py:458
  219.0 0.8 copy.73.col_ref
  219.8 0.6 copy-done.1
  220.4 20.8 %velocity_step.1 = (f32[3,4,256,512]{3,2,1,0:T(8,128)}, f32[256,24]{1,0:T(8,128)}, f32[3,4,512]{2,1,0:T(4,128)}, f32[3,4,512]{2,1,0:T(4,128)}) custom-call(f32[6,4,256,512]{3,2,1,0:T(8,128)} %s_ref.3, f32[6,4,256,512]{3,2,1,0:T(8,128)} %s_ref.3, f32[6,4,256,512]{3,2,1,0:T(8,128)} %s_ref.3, f32[3,4,512]{2,1,0:T(4,128)} %copy-done.1, f32[3,4,512]{2,1,0:T(4,128)} %copy-done.2, ...), custom_call_target="tpu_custom_call" | custom-call | flops 10000000 | bytes 25165824 | tf_op jit(solution)/shard_map/velocity_step/pallas_call | solution.py:540
  241.2 1.1 fusion.15
  242.3 6.3 %collective-permute-start.6 = (f32[256,12]{1,0:T(8,128)S(1)}, f32[256,12]{1,0:T(8,128)S(1)}, u32[]{:S(2)}, u32[]{:S(2)}) collective-permute-start(f32[256,12]{1,0:T(8,128)S(1)} %get-tuple-element.29), channel_id=1, source_target_pairs={{0,1},{1,2},{2,3},{3,0},{4,5},{5,6},{6,7},{7,4},{8,9},{9,10},{10,1... | collective-permute-start | bytes 36872 | tf_op jit(solution)/shard_map/ppermute | solution.py:270
  248.6 1.5 collective-permute-start.7
  250.3 2.5 collective-permute-start.5
  252.7 1.7 collective-permute-done.6
  254.4 2.5 collective-permute-done.7
  257.0 0.8 pad_maximum_fusion.col_ref
  257.7 0.6 copy-done.3
  258.3 17.5 %stress_step.1 = f32[6,4,256,512]{3,2,1,0:T(8,128)} custom-call(f32[3,4,256,512]{3,2,1,0:T(8,128)} %get-tuple-element.4.v_ref.prev_ref.next_ref, f32[3,4,256,512]{3,2,1,0:T(8,128)} %get-tuple-element.4.v_ref.prev_ref.next_ref, f32[3,4,256,512]{3,2,1,0:T(8,128)} %get-tuple-element.4.v_ref.prev_ref.next_ref, f32[3,4,512]{2,1,0:T(4,128)} %copy-done.3, ...), custom_call_target="tpu_custom_call" | custom-call | flops 20000000 | bytes 31457280 | tf_op jit(solution)/shard_map/stress_step/pallas_call | solution.py:565
  (33 shorter events, 1.6 us)
Async XLA Ops:
  1.7 218.0 %collective-permute-start = (f32[3,4,512]{2,1,0:T(4,128)S(1)}, f32[3,4,512]{2,1,0:T(4,128)S(1)}, u32[]{:S(2)}, u32[]{:S(2)}) collective-permute-start(f32[3,4,512]{2,1,0:T(4,128)S(1)} %pad_maximum_fusion.1), channel_id=1, source_target_pairs={{0,4},{4,8},{8,12},{12,16},{16,20},{20,24},{24,28},{28,0},{1,5},{5... | collective-permute-start | bytes 73736 | tf_op jit(solution)/shard_map/ppermute | solution.py:270
  2.3 217.5 %collective-permute-start.1 = (f32[3,4,512]{2,1,0:T(4,128)S(1)}, f32[3,4,512]{2,1,0:T(4,128)S(1)}, u32[]{:S(2)}, u32[]{:S(2)}) collective-permute-start(f32[3,4,512]{2,1,0:T(4,128)S(1)} %pad_maximum_fusion.2), channel_id=1, source_target_pairs={{4,0},{8,4},{12,8},{16,12},{20,16},{24,20},{28,24},{0,28},{5,1},{9... | collective-permute-start | bytes 73736 | tf_op jit(solution)/shard_map/ppermute | solution.py:270
  8.3 210.7 %collective-permute-start.3 = (f32[256,12]{0,1:T(8,128)S(1)}, f32[256,12]{0,1:T(8,128)S(1)}, u32[]{:S(2)}, u32[]{:S(2)}) collective-permute-start(f32[256,12]{0,1:T(8,128)S(1)} %maximum_bitcast_fusion.1), channel_id=1, source_target_pairs={{1,0},{2,1},{3,2},{0,3},{5,4},{6,5},{7,6},{4,7},{9,8},{10,9},{11,1... | collective-permute-start | bytes 36872 | tf_op jit(solution)/shard_map/ppermute | solution.py:270
  13.2 205.7 %collective-permute-start.2 = (f32[256,12]{0,1:T(8,128)S(1)}, f32[256,12]{0,1:T(8,128)S(1)}, u32[]{:S(2)}, u32[]{:S(2)}) collective-permute-start(f32[256,12]{0,1:T(8,128)S(1)} %maximum_bitcast_fusion), channel_id=1, source_target_pairs={{0,1},{1,2},{2,3},{3,0},{4,5},{5,6},{6,7},{7,4},{8,9},{9,10},{10,1... | collective-permute-start | bytes 36872 | tf_op jit(solution)/shard_map/ppermute | solution.py:270
  32.9 2.6 copy-start
  219.8 0.6 copy-start.1
  219.8 0.6 copy-start.2
  242.3 12.2 %collective-permute-start.6 = (f32[256,12]{1,0:T(8,128)S(1)}, f32[256,12]{1,0:T(8,128)S(1)}, u32[]{:S(2)}, u32[]{:S(2)}) collective-permute-start(f32[256,12]{1,0:T(8,128)S(1)} %get-tuple-element.29), channel_id=1, source_target_pairs={{0,1},{1,2},{2,3},{3,0},{4,5},{5,6},{6,7},{7,4},{8,9},{9,10},{10,1... | collective-permute-start | bytes 36872 | tf_op jit(solution)/shard_map/ppermute | solution.py:270
  248.6 8.4 %collective-permute-start.7 = (f32[256,12]{1,0:T(8,128)S(1)}, f32[256,12]{1,0:T(8,128)S(1)}, u32[]{:S(2)}, u32[]{:S(2)}) collective-permute-start(f32[256,12]{1,0:T(8,128)S(1)} %get-tuple-element.30), channel_id=1, source_target_pairs={{1,0},{2,1},{3,2},{0,3},{5,4},{6,5},{7,6},{4,7},{9,8},{10,9},{11,1... | collective-permute-start | bytes 36872 | tf_op jit(solution)/shard_map/ppermute | solution.py:270
  250.1 7.6 %collective-permute-start.4 = (f32[3,4,512]{2,1,0:T(4,128)}, f32[3,4,512]{2,1,0:T(4,128)S(1)}, u32[]{:S(2)}, u32[]{:S(2)}) collective-permute-start(f32[3,4,512]{2,1,0:T(4,128)} %get-tuple-element.7), channel_id=1, source_target_pairs={{0,4},{4,8},{8,12},{12,16},{16,20},{20,24},{24,28},{28,0},{1,5},{5... | collective-permute-start | bytes 73736 | tf_op jit(solution)/shard_map/ppermute | solution.py:270
  250.3 7.4 %collective-permute-start.5 = (f32[3,4,512]{2,1,0:T(4,128)}, f32[3,4,512]{2,1,0:T(4,128)S(1)}, u32[]{:S(2)}, u32[]{:S(2)}) collective-permute-start(f32[3,4,512]{2,1,0:T(4,128)} %get-tuple-element.8), channel_id=1, source_target_pairs={{4,0},{8,4},{12,8},{16,12},{20,16},{24,20},{28,24},{0,28},{5,1},{9... | collective-permute-start | bytes 73736 | tf_op jit(solution)/shard_map/ppermute | solution.py:270
  257.7 0.6 copy-start.3
  257.7 0.6 copy-start.4
where the time goes:
time: 276 us
  Pallas kernels  221 us (80%)
  local copies, waits for them, and re-layouts  22.8 us (8%)
  starting transfers between devices  18.4 us (7%)
  other arithmetic  8.78 us (3%)
  waiting for transfers between devices  4.24 us (2%)
    pallas_call x1, Pallas kernels, fault_traction(): pl.pallas_call(partial(fault_kernel, scale), out_shape=struct(face.shape)...  182 us
    pallas_call x1, Pallas kernels, local(): pl.pallas_call(velocity_step, grid=grid, in_specs=[tile_spec(stress.shape...  20.8 us
    pallas_call x1, Pallas kernels, local(): pl.pallas_call(stress_step, grid=grid, in_specs=[tile_spec(velocity.shape...  17.5 us
    ppermute x4, starting transfers between devices, edges(): lax.ppermute(first, axis, backward)  11.3 us
    transpose x1, other arithmetic, local(): past = past.reshape(2, 3, modes, dip_count, width).transpose(1, 0, 3, 2, 4)  7.91 us
    slice x1, local copies, waits for them, and re-layouts, local(): strike_table = dip_table[:, :, ::width // cells, :cells]  7.12 us
    ppermute x4, starting transfers between devices, edges(): lax.ppermute(last, axis, forward)  7.11 us
  transfers between devices with their start and end apart: 8, of which 2 were waited for; matrix products, arithmetic and copies ran while one was open for 10% of the time, Pallas kernels for 66%

commit v1 on v0

--- a/solution.py
+++ b/solution.py
@@ -111,7 +111,7 @@
             o_ref[s, z] = held[z, pl.ds(s * rows, rows), :]
 
 
-def dip_response(scale, x_refs, tw_ref, table_ref, now_ref, past_ref, o_refs, held):
+def dip_forward(x_refs, tw_ref, table_ref, weight_ref, past_ref, held):
     count, _, rows, width = x_refs[0].shape
     for h, x_ref in enumerate(x_refs):
         part = slice(h * width, (h + 1) * width)
@@ -127,10 +127,14 @@
             held[0, pl.ds(l * rows, rows), part] = real_part * cos + imag_part * sin
             held[1, pl.ds(l * rows, rows), part] = imag_part * cos - real_part * sin
     real_part, imag_part = complex_product(held[0], held[1], table_ref, -1.0, False)
-    weight = scale * now_ref[...]
-    real_part = weight * real_part + past_ref[0]
-    imag_part = weight * imag_part + past_ref[1]
-    real_part, imag_part = complex_product(real_part, imag_part, table_ref, 1.0, False)
+    weight = weight_ref[...]
+    held[0] = weight * real_part + past_ref[0]
+    held[1] = weight * imag_part + past_ref[1]
+
+
+def dip_inverse(held, tw_ref, table_ref, o_refs):
+    count, _, rows, width = o_refs[0].shape
+    real_part, imag_part = complex_product(held[0], held[1], table_ref, 1.0, False)
     held[0] = real_part
     held[1] = imag_part
     for l in range(count):
@@ -171,55 +175,19 @@
     return 0.5 * (high - low)
 
 
-def strike_edges(low_ref, prev_ref, high_ref, next_ref, slot, component, z):
+def stress_step(v_ref, prev_ref, next_ref, row_ref, col_ref, w_ref, s_ref, y_ref, n_ref, o_ref):
+    layers = v_ref.shape[1]
     i, last = pl.program_id(0), pl.num_programs(0) - 1
-    before = jnp.where(i == 0, low_ref[slot, z : z + 1, :], prev_ref[component, z, 7:8, :])
-    after = jnp.where(i == last, high_ref[slot, z : z + 1, :], next_ref[component, z, 0:1, :])
-    return before, after
-
-
-def velocity_step(s_ref, prev_ref, next_ref, low_ref, high_ref, col_ref, v_ref, t_ref, o_ref, c_ref, l_ref, h_ref):
-    layers = v_ref.shape[1]
-    width = v_ref.shape[3]
-    half = 3 * layers
-    for component, (sx, sy, sz) in enumerate(((0, 3, 4), (3, 1, 5), (4, 5, 2))):
-        for z in range(layers):
-            before, after = strike_edges(low_ref, prev_ref, high_ref, next_ref, component, sx, z)
-            total = rows_diff(s_ref[sx, z], before, after)
-            k = component * layers + z
-            total = total + cols_diff(
-                s_ref[sy, z], col_ref[:, k : k + 1], col_ref[:, half + k : half + k + 1]
-            )
-            low = t_ref[component] if z == 0 else s_ref[sz, z - 1]
-            if z + 1 < layers:
-                total = total + 0.5 * (s_ref[sz, z + 1] - low)
-            else:
-                total = total - 0.5 * low
-            value = v_ref[component, z] + COURANT * total
-            o_ref[component, z] = value
-            c_ref[:, k : k + 1] = value[:, 0:1]
-            c_ref[:, half + k : half + k + 1] = value[:, width - 1 : width]
-
-            @pl.when(pl.program_id(0) == 0)
-            def _():
-                l_ref[component, z : z + 1, :] = value[0:1, :]
-
-            @pl.when(pl.program_id(0) == pl.num_programs(0) - 1)
-            def _():
-                h_ref[component, z : z + 1, :] = value[-1:, :]
-
-
-def stress_step(v_ref, prev_ref, next_ref, low_ref, high_ref, col_ref, w_ref, s_ref, y_ref, o_ref):
-    layers = v_ref.shape[1]
-    half = 3 * layers
+    n_ref[...] = v_ref[...]
     for z in range(layers):
         dx, dy, dz = [], [], []
         for c in range(3):
-            before, after = strike_edges(low_ref, prev_ref, high_ref, next_ref, c, c, z)
+            before = jnp.where(i == 0, row_ref[0, c, z, 7:8, :], prev_ref[c, z, 7:8, :])
+            after = jnp.where(i == last, row_ref[1, c, z, 0:1, :], next_ref[c, z, 0:1, :])
             k = c * layers + z
             dx.append(rows_diff(v_ref[c, z], before, after))
             dy.append(
-                cols_diff(v_ref[c, z], col_ref[:, k : k + 1], col_ref[:, half + k : half + k + 1])
+                cols_diff(v_ref[c, z], col_ref[0, :, k : k + 1], col_ref[1, :, k : k + 1])
             )
             low = w_ref[c] if z == 0 else v_ref[c, z - 1]
             if z + 1 < layers:
@@ -259,27 +227,20 @@
     return pl.CostEstimate(flops=int(flops), bytes_accessed=int(moved), transcendentals=0)
 
 
-def ring(axis):
-    count = lax.axis_size(axis)
-    forward = [(i, (i + 1) % count) for i in range(count)]
-    return forward, [(b, a) for a, b in forward]
-
-
-def edges(first, last, axis):
-    forward, backward = ring(axis)
-    return lax.ppermute(last, axis, forward), lax.ppermute(first, axis, backward)
-
-
 def fault_kernel(
     scale,
     face_ref,
-    strike_tw_ref,
+    turns_ref,
     strike_table_ref,
     dip_tw_ref,
     dip_table_ref,
-    now_ref,
-    past_ref,
-    o_ref,
+    kernel_ref,
+    history_ref,
+    velocity_ref,
+    stress_ref,
+    v_ref,
+    row_ref,
+    col_ref,
     x1,
     b1,
     b2,
@@ -287,15 +248,36 @@
     t2,
     u1,
     u2,
-    w1,
     w2,
-    y1,
     held,
     held_part,
+    weight,
+    strike_tw_ref,
+    lags,
+    lag_held,
+    past_ref,
+    lag_sem,
+    past_sem,
     send_sem,
     recv_sem,
+    mirror_sem,
+    o_ref,
+    v_held,
+    stress_held,
+    edge_held,
+    row_in,
+    col_out,
+    col_in,
+    col_new,
+    top_out,
+    top_in,
+    slab_sem,
+    tile_sem,
+    edge_sem,
+    edge_recv,
 ):
     count, narrow = x1.shape[0], x1.shape[-1]
+    w1, y1, now_ref = b1, x1, lags.at[0]
     parts = count // past_ref.shape[0]
     sizes = {"bx": lax.axis_size("bx"), "by": lax.axis_size("by")}
     place = {"bx": lax.axis_index("bx"), "by": lax.axis_index("by")}
@@ -305,7 +287,47 @@
             return (target, place["by"])
         return (place["bx"], target)
 
+    strike, dip = place["bx"], place["by"]
+    modes, zone = t2.shape[3], min(8, t2.shape[3])
+
+    def active(target):
+        return lax.rem(strike + target, 2) == 0
+
+    full = active(dip)
+    thin = jnp.logical_and(jnp.logical_not(full), strike == 0)
+    forward = jnp.logical_or(full, strike == 0)
+    mirror = (lax.rem(sizes["bx"] - strike, sizes["bx"]), sizes["by"] - 1 - dip)
+
+    @pl.when(thin)
+    def _():
+        @pl.loop(0, count)
+        def _(g):
+            t2[g] = jnp.zeros(t2.shape[1:], F32)
+
+    layers, cells, width = v_held.shape[1:]
+    components = past_ref.shape[0]
+    lag_loads = [
+        pltpu.make_async_copy(
+            kernel_ref.at[:, :, 0, l, :], lags.at[:, pl.ds(l * modes, modes), :], lag_sem.at[l]
+        )
+        for l in range(sizes["by"])
+    ]
+
+    def past_loads(i):
+        slot = lax.rem(i, 2)
+        return [
+            pltpu.make_async_copy(
+                history_ref.at[:, slot, lax.div(i, 2), :, 0, l, :],
+                lag_held.at[slot, :, pl.ds(l * modes, modes), :],
+                past_sem.at[slot, l],
+            )
+            for l in range(sizes["by"])
+        ]
+
+    for load in lag_loads:
+        load.start()
     barrier = pltpu.get_barrier_semaphore()
+    pl.semaphore_signal(barrier, 1, device_id=mirror, device_id_type=pl.DeviceIdType.MESH)
     for axis in ("bx", "by"):
 
         @pl.loop(1, sizes[axis])
@@ -315,7 +337,17 @@
                 barrier, 1, device_id=device(axis, target), device_id_type=pl.DeviceIdType.MESH
             )
 
-    pl.semaphore_wait(barrier, sizes["bx"] + sizes["by"] - 2)
+    pl.semaphore_wait(barrier, sizes["bx"] + sizes["by"] - 1)
+
+    swap = pltpu.make_async_remote_copy(
+        src_ref=weight,
+        dst_ref=weight,
+        send_sem=mirror_sem.at[0],
+        recv_sem=mirror_sem.at[1],
+        device_id=mirror,
+        device_id_type=pl.DeviceIdType.MESH,
+    )
+
 
     def piece(ref, g, slot):
         if len(ref.shape) == 4 and ref.shape[0] != count:
@@ -356,6 +388,67 @@
         def _(k):
             copy(stage, axis, c, k, source, landing).wait()
 
+    def tile(ref, g, slot):
+        return ref.at[g, slot, :, pl.ds(0, zone), :]
+
+    def lean(g, k):
+        target = lax.rem(dip + k, sizes["by"])
+        return pltpu.make_async_remote_copy(
+            src_ref=tile(t1, g, target),
+            dst_ref=tile(t2, g, dip),
+            send_sem=send_sem.at[2, g, k],
+            recv_sem=recv_sem.at[2, g, k],
+            device_id=device("by", target),
+            device_id_type=pl.DeviceIdType.MESH,
+        )
+
+    def lean_own(g):
+        return pltpu.make_async_copy(tile(t1, g, dip), tile(t2, g, dip), recv_sem.at[2, g, 0])
+
+    def each_forward(g, whole, part):
+        @pl.loop(1, sizes["by"])
+        def _(k):
+            wanted = active(lax.rem(dip + k, sizes["by"]))
+
+            @pl.when(wanted)
+            def _():
+                whole(copy(2, "by", g, k, t1, t2))
+
+            @pl.when(jnp.logical_and(jnp.logical_not(wanted), strike == 0))
+            def _():
+                part(lean(g, k))
+
+    def spread(g):
+        each_forward(g, lambda c: c.start(), lambda c: c.start())
+
+        @pl.when(full)
+        def _():
+            own(2, "by", g, t1, t2).start()
+
+        @pl.when(thin)
+        def _():
+            lean_own(g).start()
+
+    def spread_end(g):
+        each_forward(g, lambda c: c.wait_send(), lambda c: c.wait_send())
+
+    def gather(g):
+        @pl.when(full)
+        def _():
+            own(2, "by", g, t1, t2).wait()
+
+            @pl.loop(1, sizes["by"])
+            def _(k):
+                copy(2, "by", g, k, t1, t2).wait_recv()
+
+        @pl.when(thin)
+        def _():
+            lean_own(g).wait()
+
+            @pl.loop(1, sizes["by"])
+            def _(k):
+                lean(g, k).wait_recv()
+
     stages = (
         ("bx", face_ref, x1),
         ("bx", b1, b2),
@@ -381,7 +474,7 @@
     def across(g):
         take(1, g)
         strike_cells_dft(-1.0, b2.at[g], strike_tw_ref, strike_table_ref, t1.at[g], held_part)
-        go(2, g)
+        spread(g)
 
     def back(g):
         take(3, g)
@@ -393,56 +486,354 @@
         strike_inverse(sizes["bx"], scale, w2.at[g], y1.at[g])
         go(5, g)
 
-    go(0, 0)
-    go(0, 1)
-
-    @pl.loop(0, count + 1)
-    def _(g):
-        @pl.when(g < count)
-        def _():
-            enter(g)
-
-        @pl.when(g + 2 < count)
-        def _():
-            go(0, g + 2)
-
-        @pl.when(g > 0)
-        def _():
-            across(g - 1)
-
-    @pl.loop(0, past_ref.shape[0])
-    def _(c):
-        for h in range(parts):
-            take(2, c * parts + h)
-        dip_response(
-            scale,
-            [t2.at[c * parts + h] for h in range(parts)],
+    def remember(i):
+        for load in past_loads(i):
+            load.wait()
+        slot = lax.rem(i, 2)
+
+        @pl.loop(0, cells // 8)
+        def _(k):
+            rows = pl.ds(pl.multiple_of(k * 8, 8), 8)
+            total = lags[1, rows, :] * lag_held[slot, 0, rows, :]
+            for h in range(1, lag_held.shape[1]):
+                total = total + lags[h + 1, rows, :] * lag_held[slot, h, rows, :]
+            past_ref[lax.div(i, 2), slot, rows, :] = total
+
+        @pl.when(i + 2 < 2 * components)
+        def _():
+            for load in past_loads(i + 2):
+                load.start()
+
+    def pick(rows, columns, total, wrap):
+        at = lax.broadcasted_iota(jnp.int32, (rows, columns), 0)
+        at = at + lax.broadcasted_iota(jnp.int32, (rows, columns), 1)
+        at = jnp.where(at == total, 1.0, jnp.where(at == wrap, 1.0, 0.0))
+        return at.astype(BF16)
+
+    def place_all(value, table, left):
+        total = None
+        for _ in range(3):
+            piece = value.astype(BF16)
+            value = value - piece.astype(F32)
+            a, b = (table, piece) if left else (piece, table)
+            term = lax.dot_general(a, b, (((1,), (0,)), ((), ())), preferred_element_type=F32)
+            total = term if total is None else total + term
+        return total
+
+    def mirrored():
+        flip = pick(modes, modes, jnp.where(strike == 0, modes, modes - 1), -1)
+        for l in range(sizes["by"]):
+            other = (sizes["by"] - l) % sizes["by"]
+            table = pick(width, width, width if l == 0 else width - 1, 0 if l == 0 else -1)
+            value = place_all(now_ref[pl.ds(l * modes, modes), :], table, False)
+            weight[pl.ds(other * modes, modes), :] = place_all(value, flip, True)
+
+    def weigh():
+        @pl.when(full)
+        def _():
+            swap.wait_recv()
+            weight[...] = scale * (now_ref[...] + weight[...])
+
+        @pl.when(thin)
+        def _():
+            swap.wait_send()
+            row = lax.broadcasted_iota(jnp.int32, now_ref.shape, 0)
+            weight[...] = jnp.where(lax.rem(row, modes) == 0, scale * now_ref[...], 0.0)
+
+    def respond(c):
+        @pl.when(forward)
+        def _():
+            for h in range(parts):
+                gather(c * parts + h)
+            dip_forward(
+                [t2.at[c * parts + h] for h in range(parts)],
+                dip_tw_ref,
+                dip_table_ref,
+                weight,
+                past_ref.at[c],
+                held,
+            )
+
+        @pl.when(jnp.logical_not(forward))
+        def _():
+            held[...] = past_ref[c]
+
+        dip_inverse(
+            held,
             dip_tw_ref,
             dip_table_ref,
-            now_ref,
-            past_ref.at[c],
             [u1.at[c * parts + h] for h in range(parts)],
-            held,
         )
         for h in range(parts):
             go(3, c * parts + h)
 
-    @pl.loop(0, count + 1)
-    def _(g):
-        @pl.when(g < count)
-        def _():
-            back(g)
-
-        @pl.when(g > 0)
-        def _():
-            leave(g - 1)
+    for load in past_loads(0) + past_loads(1):
+        load.start()
+    size = stress_held.shape[3] - 16
+    tiles = cells // size
+    block = col_out.shape[2]
+    sources = ((0, 3, 4), (3, 1, 5), (4, 5, 2))
+    up = {axis: lax.rem(place[axis] + 1, sizes[axis]) for axis in sizes}
+    down = {axis: lax.rem(place[axis] + sizes[axis] - 1, sizes[axis]) for axis in sizes}
+
+    def pair(axis, first, last, low, high, slot):
+        return [
+            pltpu.make_async_remote_copy(
+                src_ref=source,
+                dst_ref=landing,
+                send_sem=edge_sem.at[slot + i],
+                recv_sem=edge_recv.at[slot + i],
+                device_id=device(axis, target[axis]),
+                device_id_type=pl.DeviceIdType.MESH,
+            )
+            for i, (source, landing, target) in enumerate(((last, low, up), (first, high, down)))
+        ]
+
+    stress_rows = []
+    for k, c in enumerate(sources[0]):
+        stress_rows += pair(
+            "bx",
+            stress_ref.at[c, :, pl.ds(0, 8), :],
+            stress_ref.at[c, :, pl.ds(cells - 8, 8), :],
+            row_in.at[0, k],
+            row_in.at[1, k],
+            2 * k,
+        )
+    stress_cols = pair("by", col_out.at[0], col_out.at[1], col_in.at[0], col_in.at[1], 6)
+    deep = pl.ds(1, layers - 1)
+    deep_rows, top_rows = [
+        pair(
+            "bx",
+            v_held.at[:, z, pl.ds(0, 8), :],
+            v_held.at[:, z, pl.ds(cells - 8, 8), :],
+            row_ref.at[0, :, z],
+            row_ref.at[1, :, z],
+            slot,
+        )
+        for z, slot in ((deep, 8), (0, 12))
+    ]
+    top_cols = pair("by", top_out.at[0], top_out.at[1], top_in.at[0], top_in.at[1], 14)
+    new_cols = pair("by", col_new.at[0], col_new.at[1], col_ref.at[0], col_ref.at[1], 10)
+    sides = (pl.ds(0, block), pl.ds(width - block, block))
+    edge_loads = [
+        pltpu.make_async_copy(
+            stress_ref.at[c, :, :, side], edge_held.at[i, k], slab_sem.at[3 * i + k]
+        )
+        for i, side in enumerate(sides)
+        for k, c in enumerate(sources[1])
+    ]
+    velocity_load = pltpu.make_async_copy(velocity_ref, v_held, slab_sem.at[6])
+    deep_store = pltpu.make_async_copy(v_held.at[:, deep], v_ref.at[:, deep], slab_sem.at[7])
+    top_store = pltpu.make_async_copy(v_held.at[:, 0], v_ref.at[:, 0], slab_sem.at[8])
+
+    def tile_loads(t):
+        slot = lax.rem(t, 2)
+        row = pl.multiple_of(t * size, 8)
+        before = pl.multiple_of(jnp.maximum(row - 8, 0), 8)
+        after = pl.multiple_of(jnp.minimum(row + size, cells - 8), 8)
+        loads = [
+            pltpu.make_async_copy(
+                stress_ref.at[:, :, pl.ds(row, size), :],
+                stress_held.at[slot, :, :, pl.ds(8, size), :],
+                tile_sem.at[slot, 0],
+            )
+        ]
+        for k, c in enumerate(sources[0]):
+            for i, (source, landing) in enumerate(((before, 0), (after, size + 8))):
+                loads.append(
+                    pltpu.make_async_copy(
+                        stress_ref.at[c, :, pl.ds(source, 8), :],
+                        stress_held.at[slot, c, :, pl.ds(landing, 8), :],
+                        tile_sem.at[slot, 1 + 2 * k + i],
+                    )
+                )
+        return loads
+
+    def edges():
+        for load in edge_loads:
+            load.wait()
+        for k in range(3):
+            for z in range(layers):
+                lane = pl.ds(k * layers + z, 1)
+                col_out[0, :, lane] = edge_held[0, k, z, :, 0:1]
+                col_out[1, :, lane] = edge_held[1, k, z, :, block - 1 : block]
+        for c in stress_cols:
+            c.start()
+
+    def slab(t):
+        @pl.when(t == 0)
+        def _():
+            velocity_load.wait()
+            for c in stress_rows + stress_cols:
+                c.wait_recv()
+
+        @pl.when(t + 1 < tiles)
+        def _():
+            for load in tile_loads(t + 1):
+                load.start()
+
+        for load in tile_loads(t):
+            load.wait()
+        slot = lax.rem(t, 2)
+        rows = pl.ds(pl.multiple_of(t * size, 8), size)
+        for component, (sx, sy, sz) in enumerate(sources):
+            for z in range(layers):
+                k = component * layers + z
+                before = jnp.where(t == 0, row_in[0, component, z, 7:8, :], stress_held[slot, sx, z, 7:8, :])
+                after = jnp.where(
+                    t == tiles - 1,
+                    row_in[1, component, z, 0:1, :],
+                    stress_held[slot, sx, z, size + 8 : size + 9, :],
+                )
+                total = rows_diff(stress_held[slot, sx, z, 8 : size + 8, :], before, after)
+                total = total + cols_diff(
+                    stress_held[slot, sy, z, 8 : size + 8, :],
+                    col_in[0, rows, k : k + 1],
+                    col_in[1, rows, k : k + 1],
+                )
+                if z + 1 < layers:
+                    total = total + 0.5 * stress_held[slot, sz, z + 1, 8 : size + 8, :]
+                if z > 0:
+                    total = total - 0.5 * stress_held[slot, sz, z - 1, 8 : size + 8, :]
+                value = v_held[component, z, rows, :] + COURANT * total
+                v_held[component, z, rows, :] = value
+                if z > 0:
+                    col_new[0, rows, k : k + 1] = value[:, 0:1]
+                    col_new[1, rows, k : k + 1] = value[:, width - 1 : width]
+
+        @pl.when(t == tiles - 1)
+        def _():
+            deep_store.start()
+            for c in deep_rows + new_cols:
+                c.start()
+
+    go(0, 0)
+    go(0, 1)
+    for load in edge_loads:
+        load.start()
+    for c in stress_rows:
+        c.start()
+    velocity_load.start()
+    for load in tile_loads(0):
+        load.start()
+    turns = turns_ref[strike]
+    strike_tw_ref[...] = jnp.concatenate([turns, jnp.zeros((block - 8, cells), F32)], axis=0).T
+    for load in lag_loads:
+        load.wait()
+    first_tile = 3
+    first_back = count + 1
+    gap = first_back + parts
+
+    def turn_of(s):
+        last, none = components - 1, components
+        whole = lax.rem(s + parts - 1, parts) == 0
+        step = lax.div(s - 1, parts)
+        now = jnp.where(jnp.logical_and(whole, step >= 2), step - 2, none)
+        now = jnp.where(now >= last, none, now)
+        now = jnp.where(s == gap + 1, last, now)
+        early = jnp.where(jnp.logical_and(whole, s > 0), step, none)
+        early = jnp.where(jnp.logical_or(s == 0, early >= last), none, early)
+        early = jnp.where(s == 0, 0, jnp.where(early == 0, none, early))
+        early = jnp.where(s == first_back + 1, last, early)
+        return jnp.where(forward, now, early)
+
+    @pl.loop(0, first_back + count + 2)
+    def _(s):
+        @pl.when(jnp.logical_and(forward, s == 2 * parts + 1))
+        def _():
+            weigh()
+
+        @pl.when(s < components)
+        def _():
+            remember(2 * s)
+            remember(2 * s + 1)
+
+        turn = turn_of(s)
+
+        @pl.when(turn < components)
+        def _():
+            respond(turn)
+
+        @pl.when(s < count)
+        def _():
+            enter(s)
+
+        @pl.when(s + 2 < count)
+        def _():
+            go(0, s + 2)
+
+        @pl.when(jnp.logical_and(s > 0, s <= count))
+        def _():
+            across(s - 1)
+
+        @pl.when(s == 0)
+        def _():
+            edges()
+
+        @pl.when(jnp.logical_and(s == 1, jnp.logical_not(full)))
+        def _():
+            mirrored()
+            swap.start()
+
+        turned = s - first_back - (s > gap).astype(jnp.int32)
+
+        @pl.when(jnp.logical_and(jnp.logical_and(turned >= 0, turned < count), s != gap))
+        def _():
+            back(turned)
+
+        done = s - first_back - 1 - (s > gap + 1).astype(jnp.int32)
+
+        @pl.when(jnp.logical_and(jnp.logical_and(done >= 0, done < count), s != gap + 1))
+        def _():
+            leave(done)
+
+        @pl.when(jnp.logical_and(s >= first_tile, s < tiles + first_tile))
+        def _():
+            slab(s - first_tile)
+
+    @pl.when(jnp.logical_not(forward))
+    def _():
+        swap.wait_send()
 
     @pl.loop(0, count)
     def _(g):
         take(5, g)
-
-
-def fault_traction(interface, now, past, tables, scale):
+        spread_end(g)
+        c = lax.div(g, parts)
+        lanes = pl.ds(pl.multiple_of(lax.rem(g, parts) * narrow, narrow), narrow)
+        high = cells // sizes["bx"]
+        for b in range(sizes["bx"]):
+            rows = pl.ds(b * high, high)
+            v_held[c, 0, rows, lanes] = v_held[c, 0, rows, lanes] - (0.5 * COURANT) * o_ref[c, b, :, lanes]
+
+    for c in top_rows:
+        c.start()
+    top_store.start()
+    lane = lax.broadcasted_iota(jnp.int32, (cells, block), 1)
+    for i, side in enumerate((0, width - block)):
+        at = block - 1 if i else 0
+        total = jnp.zeros((cells, block), F32)
+        for c in range(components):
+            value = v_held[c, 0, :, side : side + block][:, at : at + 1]
+            total = jnp.where(lane == c, value, total)
+        top_out[i] = total.T[:8]
+    for c in top_cols:
+        c.start()
+    for c in new_cols + deep_rows + top_cols:
+        c.wait_recv()
+    for i in range(2):
+        filled = jnp.concatenate([top_in[i], jnp.zeros((block - 8, cells), F32)], axis=0).T
+        for c in range(components):
+            col_ref[i, :, c * layers : c * layers + 1] = filled[:, c : c + 1]
+    deep_store.wait()
+    top_store.wait()
+    for c in stress_rows + stress_cols + new_cols + deep_rows + top_cols:
+        c.wait_send()
+    for c in top_rows:
+        c.wait()
+
+
+def fault_velocity(interface, kernel, history, tables, velocity, stress, scale):
     strike_count, dip_count = lax.axis_size("bx"), lax.axis_size("by")
     count, cells, width = interface.shape
     rows, modes = cells // strike_count, cells // dip_count
@@ -454,26 +845,53 @@
     wide = (chunks, strike_count, 2, rows, narrow)
     tall = (chunks, dip_count, 2, modes, narrow)
     peers = max(strike_count, dip_count)
-    operands = (face, *tables, now, past)
-    out = pl.pallas_call(
+    layers = velocity.shape[1]
+    tile, block = min(32, cells), min(128, width)
+    operands = (face, *tables, kernel, history, velocity, stress)
+    vmem, anywhere = pl.BlockSpec(memory_space=pltpu.VMEM), pl.BlockSpec(memory_space=pl.ANY)
+    return pl.pallas_call(
         partial(fault_kernel, scale),
-        out_shape=struct(face.shape),
-        in_specs=[pl.BlockSpec(memory_space=pltpu.VMEM)] * len(operands),
-        out_specs=pl.BlockSpec(memory_space=pltpu.VMEM),
+        out_shape=[
+            struct(velocity.shape),
+            struct((2, count, layers, 8, width)),
+            struct((2, cells, block)),
+        ],
+        in_specs=[anywhere] + [vmem] * len(tables) + [anywhere] * 4,
+        out_specs=[anywhere, vmem, vmem],
         scratch_shapes=[
-            *[pltpu.VMEM(s, F32) for s in (flat, wide, wide, tall, tall, tall, tall, wide, wide)],
-            pltpu.VMEM(flat, F32),
+            *[pltpu.VMEM(s, F32) for s in (flat, wide, wide, tall, tall, tall, tall, wide)],
             pltpu.VMEM((2, cells, width), F32),
             pltpu.VMEM((2, cells, narrow), F32),
+            pltpu.VMEM((cells, width), F32),
+            pltpu.VMEM((cells, block), F32),
+            pltpu.VMEM((kernel.shape[0], cells, width), F32),
+            pltpu.VMEM((2, history.shape[0], cells, width), F32),
+            pltpu.VMEM((count, 2, cells, width), F32),
+            pltpu.SemaphoreType.DMA((dip_count,)),
+            pltpu.SemaphoreType.DMA((2, dip_count)),
             pltpu.SemaphoreType.DMA((6, chunks, peers)),
             pltpu.SemaphoreType.DMA((6, chunks, peers)),
+            pltpu.SemaphoreType.DMA((2,)),
+            pltpu.VMEM(face.shape, F32),
+            pltpu.VMEM(velocity.shape, F32),
+            pltpu.VMEM((2, 6, layers, tile + 16, width), F32),
+            pltpu.VMEM((2, 3, layers, cells, block), F32),
+            pltpu.VMEM((2, 3, layers, 8, width), F32),
+            pltpu.VMEM((2, cells, block), F32),
+            pltpu.VMEM((2, cells, block), F32),
+            pltpu.VMEM((2, cells, block), F32),
+            pltpu.VMEM((2, 8, cells), F32),
+            pltpu.VMEM((2, 8, cells), F32),
+            pltpu.SemaphoreType.DMA((9,)),
+            pltpu.SemaphoreType.DMA((2, 7)),
+            pltpu.SemaphoreType.DMA((16,)),
+            pltpu.SemaphoreType.DMA((16,)),
         ],
         compiler_params=pltpu.CompilerParams(
-            collective_id=0, has_side_effects=True, vmem_limit_bytes=60 * 1024 * 1024
+            collective_id=0, has_side_effects=True, vmem_limit_bytes=63 * 1024 * 1024
         ),
-        name="fault_traction",
+        name="fault_velocity",
     )(*operands)
-    return out.reshape(count, cells, width)
 
 
 def tile_spec(shape, tile):
@@ -497,90 +915,36 @@
     _, layers, cells, width = velocity.shape
     strike_length, dip_length = cells * strike_count, width * dip_count
     scale = 1.0 / math.sqrt(strike_length * dip_length)
-    angle = (2.0 * math.pi / strike_length) * (
-        jnp.arange(cells, dtype=jnp.int32) * lax.axis_index("bx")
-    ).astype(F32)
-    strike_tw = jnp.stack([jnp.cos(angle), jnp.sin(angle)], axis=1)
+    turn = np.outer(np.arange(strike_count), np.arange(cells)) * (2.0 * math.pi / strike_length)
+    turns = np.zeros((strike_count, 8, cells), np.float32)
+    turns[:, 0], turns[:, 1] = np.cos(turn), np.sin(turn)
     lane = np.outer(np.arange(dip_count), np.arange(width)) * (2.0 * math.pi / dip_length)
     dip_tw = jnp.asarray(np.stack([np.cos(lane), np.sin(lane)]).astype(np.float32))
-    dip_table = lax.optimization_barrier(square_table(width))
-    if width % cells == 0:
-        strike_table = dip_table[:, :, :: width // cells, :cells]
-    else:
-        strike_table = square_table(cells)
-    tables = (strike_tw, strike_table, dip_tw, dip_table)
-
-    past = kernel[1] * history[0]
-    for h in range(1, history.shape[0]):
-        past = past + kernel[h + 1] * history[h]
-    modes = history.shape[3]
-    past = past.reshape(2, 3, modes, dip_count, width).transpose(1, 0, 3, 2, 4)
-    past = past.reshape(3, 2, cells, width)
-    now = kernel[0].reshape(modes, dip_count, width).transpose(1, 0, 2).reshape(cells, width)
-
-    traction = fault_traction(interface_velocity, now, past, tables, scale)
-
-    tile = min(32, cells)
-    grid = (cells // tile,)
-    col_shape = (cells, 6 * layers)
-
-    def columns(first, last):
-        low, high = edges(first, last, "by")
-        return jnp.concatenate([low, high], axis=1)
-
-    def side(position):
-        flat = [stress[c, :, :, position] for c in (3, 1, 5)]
-        return jnp.concatenate(flat, axis=0).T
-
-    def line(position):
-        return jnp.stack([stress[c, :, position, :] for c in (0, 3, 4)])
-
-    cols = columns(side(0), side(width - 1))
-    low, high = edges(line(0), line(cells - 1), "bx")
-    velocity_new, new_cols, first, last = pl.pallas_call(
-        velocity_step,
-        grid=grid,
-        in_specs=[
-            tile_spec(stress.shape, tile),
-            *halo_specs(stress.shape, tile),
-            whole_block(low.shape),
-            whole_block(high.shape),
-            tile_spec(col_shape, tile),
-            tile_spec(velocity.shape, tile),
-            tile_spec(traction.shape, tile),
-        ],
-        out_specs=[
-            tile_spec(velocity.shape, tile),
-            tile_spec(col_shape, tile),
-            whole_block(low.shape),
-            whole_block(low.shape),
-        ],
-        out_shape=[struct(velocity.shape), struct(col_shape), struct(low.shape), struct(low.shape)],
-        cost_estimate=cost(1e7, stress, velocity, velocity),
-        name="velocity_step",
-    )(stress, stress, stress, low, high, cols, velocity, traction)
-    half = 3 * layers
-    cols = columns(new_cols[:, :half], new_cols[:, half:])
-    low, high = edges(first, last, "bx")
-    stress_new = pl.pallas_call(
+    dip_table = square_table(width)
+    strike_table = square_table(cells)
+    tables = (jnp.asarray(turns), strike_table, dip_tw, dip_table)
+
+    velocity_part, rows, cols = fault_velocity(
+        interface_velocity, kernel, history, tables, velocity, stress, scale
+    )
+    tile = min(64, cells)
+    return pl.pallas_call(
         stress_step,
-        grid=grid,
+        grid=(cells // tile,),
         in_specs=[
             tile_spec(velocity.shape, tile),
             *halo_specs(velocity.shape, tile),
-            whole_block(low.shape),
-            whole_block(high.shape),
-            tile_spec(col_shape, tile),
+            whole_block(rows.shape),
+            tile_spec(cols.shape, tile),
             tile_spec(interface_velocity.shape, tile),
             tile_spec(stress.shape, tile),
             tile_spec(cohesion.shape, tile),
         ],
-        out_specs=tile_spec(stress.shape, tile),
-        out_shape=struct(stress.shape),
+        out_specs=[tile_spec(velocity.shape, tile), tile_spec(stress.shape, tile)],
+        out_shape=[struct(velocity.shape), struct(stress.shape)],
         cost_estimate=cost(2e7, stress, stress, velocity),
         name="stress_step",
-    )(velocity_new, velocity_new, velocity_new, low, high, cols, interface_velocity, stress, cohesion)
-    return velocity_new, stress_new
+    )(velocity_part, velocity_part, velocity_part, rows, cols, interface_velocity, stress, cohesion)
 
 
 def solution(mesh):

time: 276 us -> 194 us (0.70)
  Pallas kernels: 221 us -> 191 us
  local copies, waits for them, and re-layouts: 22.8 us -> 0 us
  starting transfers between devices: 18.4 us -> 0 us
  other arithmetic: 8.78 us -> 0 us
  waiting for transfers between devices: 4.24 us -> 0 us
    pallas_call x3 -> x2, Pallas kernels: 221 us -> 191 us  [the longest x1 173 us: fault_velocity(): pl.pallas_call(partial(fault_kernel, scale), out_shape=[struct(velocity.s...]
    ppermute x8 -> x0, starting transfers between devices: 18.4 us -> none  [the longest x4 11.3 us: edges(): lax.ppermute(first, axis, backward)]
    slice x4 -> x0, local copies, waits for them, and re-layouts: 11.7 us -> none  [the longest x1 7.12 us: local(): strike_table = dip_table[:, :, ::width // cells, :cells]]
    transpose x3 -> x0, other arithmetic: 7.93 us -> none  [the longest x1 7.91 us: local(): past = past.reshape(2, 3, modes, dip_count, width).transpose(1, 0, 3, 2, 4)]
    ppermute x8 -> x0, waiting for transfers between devices: 4.24 us -> none  [the longest x4 2.55 us: edges(): lax.ppermute(first, axis, backward)]
    mul x1 -> x0, local copies, waits for them, and re-layouts: 3.65 us -> none  [local(): past = kernel[1] * history[0]]
    transpose x2 -> x0, local copies, waits for them, and re-layouts: 3.63 us -> none  [the longest x1 2.64 us: local(): past = past.reshape(2, 3, modes, dip_count, width).transpose(1, 0, 3, 2, 4)]
  transfers between devices with their start and end apart: 8 -> 0, of which waited for: 2 -> 0; matrix products, arithmetic and copies ran while one was open for 10% -> 0% of each run, Pallas kernels for 66% -> 0%
where the time goes in v1:
time: 194 us; the launch traced here: 191 us
  Pallas kernels  191 us (98%)
    pallas_call x1, Pallas kernels, fault_velocity(): pl.pallas_call(partial(fault_kernel, scale), out_shape=[struct(velocity.s...  173 us
    pallas_call x1, Pallas kernels, local(): pl.pallas_call(stress_step, grid=(cells // tile,), in_specs=[tile_spec(ve...  17.8 us

profile of v1, /device:TPU:0, one launch (start us, length us, event | category | flops | bytes accessed | tf_op | source)
XLA Modules:
  0.0 191.2 jit_solution(16970990097420171626)
XLA Ops:
  0.6 172.8 %fault_velocity.1 = (f32[3,4,256,512]{3,2,1,0:T(8,128)}, f32[2,3,4,8,512]{4,3,2,1,0:T(8,128)}, f32[2,256,128]{2,1,0:T(8,128)}) custom-call(f32[3,8,32,512]{3,2,1,0:T(8,128)} %bitcast.1, f32[8,8,256]{2,1,0:T(8,128)} %constant.11.clone.turns_ref, bf16[2,2,256,256]{3,2,1,0:T(8,128)(2,1)} %constant.10.clone.strike_table_ref, ...), custom_call_target="tpu_custom_call" | custom-call | tf_op jit(solution)/shard_map/fault_velocity/pallas_call | solution.py:852
  173.4 17.8 %stress_step.1 = (f32[3,4,256,512]{3,2,1,0:T(8,128)}, f32[6,4,256,512]{3,2,1,0:T(8,128)}) custom-call(f32[3,4,256,512]{3,2,1,0:T(8,128)} %get-tuple-element.5.v_ref.prev_ref.next_ref, f32[3,4,256,512]{3,2,1,0:T(8,128)} %get-tuple-element.5.v_ref.prev_ref.next_ref, f32[3,4,256,512]{3,2,1,0:T(8,128)} %get-tuple-element.5.v_ref.prev_ref.next_ref, ...), custom_call_target="tpu_custom_call" | custom-call | flops 20000000 | bytes 31457280 | tf_op jit(solution)/shard_map/stress_step/pallas_call | solution.py:931

commit v2 on v1

--- a/solution.py
+++ b/solution.py
@@ -356,14 +356,23 @@
             return ref.at[g, slot, :, pl.ds(0, narrow)]
         return ref.at[g, slot]
 
+    def several(ref, g, number):
+        if len(ref.shape) == 4 and ref.shape[0] != count:
+            lanes = pl.ds(pl.multiple_of(g % parts * narrow, narrow), narrow)
+            return ref.at[g // parts, pl.ds(0, number), :, lanes]
+        return ref.at[g, pl.ds(0, number)]
+
+    def settle(ref, sem):
+        pltpu.make_async_copy(ref, ref, sem).wait()
+
     def copy(stage, axis, c, k, source, landing):
         me = place[axis]
         target = lax.rem(me + k, sizes[axis])
         return pltpu.make_async_remote_copy(
             src_ref=piece(source, c, target),
             dst_ref=piece(landing, c, me),
-            send_sem=send_sem.at[stage, c, k],
-            recv_sem=recv_sem.at[stage, c, k],
+            send_sem=send_sem.at[stage, c],
+            recv_sem=recv_sem.at[stage, c],
             device_id=device(axis, target),
             device_id_type=pl.DeviceIdType.MESH,
         )
@@ -371,7 +380,7 @@
     def own(stage, axis, c, source, landing):
         me = place[axis]
         return pltpu.make_async_copy(
-            piece(source, c, me), piece(landing, c, me), recv_sem.at[stage, c, 0]
+            piece(source, c, me), piece(landing, c, me), recv_sem.at[stage, c]
         )
 
     def send(stage, axis, c, source, landing):
@@ -382,11 +391,8 @@
         own(stage, axis, c, source, landing).start()
 
     def receive(stage, axis, c, source, landing):
-        own(stage, axis, c, source, landing).wait()
-
-        @pl.loop(1, sizes[axis])
-        def _(k):
-            copy(stage, axis, c, k, source, landing).wait()
+        settle(several(landing, c, sizes[axis]), recv_sem.at[stage, c])
+        settle(several(landing, c, sizes[axis] - 1), send_sem.at[stage, c])
 
     def tile(ref, g, slot):
         return ref.at[g, slot, :, pl.ds(0, zone), :]
@@ -396,30 +402,27 @@
         return pltpu.make_async_remote_copy(
             src_ref=tile(t1, g, target),
             dst_ref=tile(t2, g, dip),
-            send_sem=send_sem.at[2, g, k],
-            recv_sem=recv_sem.at[2, g, k],
+            send_sem=send_sem.at[6, g],
+            recv_sem=recv_sem.at[2, g],
             device_id=device("by", target),
             device_id_type=pl.DeviceIdType.MESH,
         )
 
     def lean_own(g):
-        return pltpu.make_async_copy(tile(t1, g, dip), tile(t2, g, dip), recv_sem.at[2, g, 0])
-
-    def each_forward(g, whole, part):
+        return pltpu.make_async_copy(tile(t1, g, dip), tile(t2, g, dip), recv_sem.at[2, g])
+
+    def spread(g):
         @pl.loop(1, sizes["by"])
         def _(k):
             wanted = active(lax.rem(dip + k, sizes["by"]))
 
             @pl.when(wanted)
             def _():
-                whole(copy(2, "by", g, k, t1, t2))
+                copy(2, "by", g, k, t1, t2).start()
 
             @pl.when(jnp.logical_and(jnp.logical_not(wanted), strike == 0))
             def _():
-                part(lean(g, k))
-
-    def spread(g):
-        each_forward(g, lambda c: c.start(), lambda c: c.start())
+                lean(g, k).start()
 
         @pl.when(full)
         def _():
@@ -429,25 +432,30 @@
         def _():
             lean_own(g).start()
 
+    half = sizes["by"] // 2
+
     def spread_end(g):
-        each_forward(g, lambda c: c.wait_send(), lambda c: c.wait_send())
+        def wait(condition, number, zoned):
+            @pl.when(condition)
+            def _():
+                if zoned:
+                    settle(t1.at[g, pl.ds(0, number), :, pl.ds(0, zone), :], send_sem.at[6, g])
+                else:
+                    settle(t1.at[g, pl.ds(0, number)], send_sem.at[2, g])
+
+        wait(full, half - 1, False)
+        wait(jnp.logical_not(full), half, False)
+        wait(jnp.logical_and(full, strike == 0), half, True)
+        wait(thin, half - 1, True)
 
     def gather(g):
         @pl.when(full)
         def _():
-            own(2, "by", g, t1, t2).wait()
-
-            @pl.loop(1, sizes["by"])
-            def _(k):
-                copy(2, "by", g, k, t1, t2).wait_recv()
+            settle(t2.at[g], recv_sem.at[2, g])
 
         @pl.when(thin)
         def _():
-            lean_own(g).wait()
-
-            @pl.loop(1, sizes["by"])
-            def _(k):
-                lean(g, k).wait_recv()
+            settle(t2.at[g, :, :, pl.ds(0, zone), :], recv_sem.at[2, g])
 
     stages = (
         ("bx", face_ref, x1),
@@ -718,8 +726,6 @@
         load.start()
     turns = turns_ref[strike]
     strike_tw_ref[...] = jnp.concatenate([turns, jnp.zeros((block - 8, cells), F32)], axis=0).T
-    for load in lag_loads:
-        load.wait()
     first_tile = 3
     first_back = count + 1
     gap = first_back + parts
@@ -730,18 +736,39 @@
         step = lax.div(s - 1, parts)
         now = jnp.where(jnp.logical_and(whole, step >= 2), step - 2, none)
         now = jnp.where(now >= last, none, now)
-        now = jnp.where(s == gap + 1, last, now)
-        early = jnp.where(jnp.logical_and(whole, s > 0), step, none)
-        early = jnp.where(jnp.logical_or(s == 0, early >= last), none, early)
-        early = jnp.where(s == 0, 0, jnp.where(early == 0, none, early))
-        early = jnp.where(s == first_back + 1, last, early)
+        now = jnp.where(s == gap, last, now)
+        early = jnp.where(s == 0, 0, none)
+        early = jnp.where(s == first_back + 1, 1, early)
+        early = jnp.where(s == gap + 1, 2, early)
         return jnp.where(forward, now, early)
 
     @pl.loop(0, first_back + count + 2)
     def _(s):
+        @pl.when(s < count)
+        def _():
+            enter(s)
+
+        @pl.when(s + 2 < count)
+        def _():
+            go(0, s + 2)
+
         @pl.when(jnp.logical_and(forward, s == 2 * parts + 1))
         def _():
             weigh()
+
+        @pl.when(s == 0)
+        def _():
+            edges()
+
+        @pl.when(s == 0)
+        def _():
+            for load in lag_loads:
+                load.wait()
+
+        @pl.when(jnp.logical_and(s == 0, jnp.logical_not(full)))
+        def _():
+            mirrored()
+            swap.start()
 
         @pl.when(s < components)
         def _():
@@ -754,26 +781,9 @@
         def _():
             respond(turn)
 
-        @pl.when(s < count)
-        def _():
-            enter(s)
-
-        @pl.when(s + 2 < count)
-        def _():
-            go(0, s + 2)
-
         @pl.when(jnp.logical_and(s > 0, s <= count))
         def _():
             across(s - 1)
-
-        @pl.when(s == 0)
-        def _():
-            edges()
-
-        @pl.when(jnp.logical_and(s == 1, jnp.logical_not(full)))
-        def _():
-            mirrored()
-            swap.start()
 
         turned = s - first_back - (s > gap).astype(jnp.int32)
 
@@ -844,7 +854,6 @@
     flat = (chunks, strike_count, rows, narrow)
     wide = (chunks, strike_count, 2, rows, narrow)
     tall = (chunks, dip_count, 2, modes, narrow)
-    peers = max(strike_count, dip_count)
     layers = velocity.shape[1]
     tile, block = min(32, cells), min(128, width)
     operands = (face, *tables, kernel, history, velocity, stress)
@@ -869,8 +878,8 @@
             pltpu.VMEM((count, 2, cells, width), F32),
             pltpu.SemaphoreType.DMA((dip_count,)),
             pltpu.SemaphoreType.DMA((2, dip_count)),
-            pltpu.SemaphoreType.DMA((6, chunks, peers)),
-            pltpu.SemaphoreType.DMA((6, chunks, peers)),
+            pltpu.SemaphoreType.DMA((7, chunks)),
+            pltpu.SemaphoreType.DMA((6, chunks)),
             pltpu.SemaphoreType.DMA((2,)),
             pltpu.VMEM(face.shape, F32),
             pltpu.VMEM(velocity.shape, F32),

time: 194 us -> 181 us (0.933); the launches traced: 191 us -> 181 us
  Pallas kernels: 191 us -> 181 us
    pallas_call x1, Pallas kernels: 173 us -> 163 us  [fault_velocity(): pl.pallas_call(partial(fault_kernel, scale), out_shape=[struct(velocity.s...]
where the time goes in v2:
time: 181 us
  Pallas kernels  181 us (100%)
    pallas_call x1, Pallas kernels, fault_velocity(): pl.pallas_call(partial(fault_kernel, scale), out_shape=[struct(velocity.s...  163 us
    pallas_call x1, Pallas kernels, local(): pl.pallas_call(stress_step, grid=(cells // tile,), in_specs=[tile_spec(ve...  17.8 us

profile of v2, /device:TPU:0, one launch (start us, length us, event | category | flops | bytes accessed | tf_op | source)
XLA Modules:
  0.0 181.2 jit_solution(13003604936635924461)
XLA Ops:
  0.6 162.7 %fault_velocity.1 = (f32[3,4,256,512]{3,2,1,0:T(8,128)}, f32[2,3,4,8,512]{4,3,2,1,0:T(8,128)}, f32[2,256,128]{2,1,0:T(8,128)}) custom-call(f32[3,8,32,512]{3,2,1,0:T(8,128)} %bitcast.1, f32[8,8,256]{2,1,0:T(8,128)} %constant.11.clone.turns_ref, bf16[2,2,256,256]{3,2,1,0:T(8,128)(2,1)} %constant.10.clone.strike_table_ref, ...), custom_call_target="tpu_custom_call" | custom-call | tf_op jit(solution)/shard_map/fault_velocity/pallas_call | solution.py:861
  163.4 17.8 %stress_step.1 = (f32[3,4,256,512]{3,2,1,0:T(8,128)}, f32[6,4,256,512]{3,2,1,0:T(8,128)}) custom-call(f32[3,4,256,512]{3,2,1,0:T(8,128)} %get-tuple-element.5.v_ref.prev_ref.next_ref, f32[3,4,256,512]{3,2,1,0:T(8,128)} %get-tuple-element.5.v_ref.prev_ref.next_ref, f32[3,4,256,512]{3,2,1,0:T(8,128)} %get-tuple-element.5.v_ref.prev_ref.next_ref, ...), custom_call_target="tpu_custom_call" | custom-call | flops 20000000 | bytes 31457280 | tf_op jit(solution)/shard_map/stress_step/pallas_call | solution.py:940

commit v3 on v2

--- a/solution.py
+++ b/solution.py
@@ -164,7 +164,7 @@
     row = lax.broadcasted_iota(jnp.int32, value.shape, 0)
     low = jnp.where(row == 0, before, pltpu.roll(value, 1, 0))
     high = jnp.where(row == count - 1, after, pltpu.roll(value, count - 1, 0))
-    return 0.5 * (high - low)
+    return high - low
 
 
 def cols_diff(value, before, after):
@@ -172,7 +172,7 @@
     col = lax.broadcasted_iota(jnp.int32, value.shape, 1)
     low = jnp.where(col == 0, before, pltpu.roll(value, 1, 1))
     high = jnp.where(col == count - 1, after, pltpu.roll(value, count - 1, 1))
-    return 0.5 * (high - low)
+    return high - low
 
 
 def stress_step(v_ref, prev_ref, next_ref, row_ref, col_ref, w_ref, s_ref, y_ref, n_ref, o_ref):
@@ -191,17 +191,18 @@
             )
             low = w_ref[c] if z == 0 else v_ref[c, z - 1]
             if z + 1 < layers:
-                dz.append(0.5 * (v_ref[c, z + 1] - low))
+                dz.append(v_ref[c, z + 1] - low)
             else:
-                dz.append(-0.5 * low)
+                dz.append(-low)
+        step = 0.5 * COURANT
         dilation = dx[0] + dy[1] + dz[2]
-        xx = s_ref[0, z] + COURANT * (dilation + 2.0 * dx[0])
-        yy = s_ref[1, z] + COURANT * (dilation + 2.0 * dy[1])
-        zz = s_ref[2, z] + COURANT * (dilation + 2.0 * dz[2])
-        xy = s_ref[3, z] + COURANT * (dy[0] + dx[1])
-        xz = s_ref[4, z] + COURANT * (dz[0] + dx[2])
-        yz = s_ref[5, z] + COURANT * (dz[1] + dy[2])
-        pressure = (xx + yy + zz) / 3.0
+        xx = s_ref[0, z] + step * (dilation + 2.0 * dx[0])
+        yy = s_ref[1, z] + step * (dilation + 2.0 * dy[1])
+        zz = s_ref[2, z] + step * (dilation + 2.0 * dz[2])
+        xy = s_ref[3, z] + step * (dy[0] + dx[1])
+        xz = s_ref[4, z] + step * (dz[0] + dx[2])
+        yz = s_ref[5, z] + step * (dz[1] + dy[2])
+        pressure = (xx + yy + zz) * (1.0 / 3.0)
         xx, yy, zz = xx - pressure, yy - pressure, zz - pressure
         shear = jnp.sqrt(0.5 * (xx * xx + yy * yy + zz * zz) + (xy * xy + xz * xz + yz * yz))
         limit = y_ref[z] + FRICTION * jnp.maximum(-pressure, 0.0)
@@ -298,12 +299,6 @@
     forward = jnp.logical_or(full, strike == 0)
     mirror = (lax.rem(sizes["bx"] - strike, sizes["bx"]), sizes["by"] - 1 - dip)
 
-    @pl.when(thin)
-    def _():
-        @pl.loop(0, count)
-        def _(g):
-            t2[g] = jnp.zeros(t2.shape[1:], F32)
-
     layers, cells, width = v_held.shape[1:]
     components = past_ref.shape[0]
     lag_loads = [
@@ -392,7 +387,6 @@
 
     def receive(stage, axis, c, source, landing):
         settle(several(landing, c, sizes[axis]), recv_sem.at[stage, c])
-        settle(several(landing, c, sizes[axis] - 1), send_sem.at[stage, c])
 
     def tile(ref, g, slot):
         return ref.at[g, slot, :, pl.ds(0, zone), :]
@@ -474,6 +468,10 @@
         axis, source, landing = stages[stage]
         receive(stage, axis, g, source, landing)
 
+    def sent(stage, g):
+        axis, source, landing = stages[stage]
+        settle(several(landing, g, sizes[axis] - 1), send_sem.at[stage, g])
+
     def enter(g):
         take(0, g)
         strike_forward(sizes["bx"], x1.at[g], b1.at[g])
@@ -486,6 +484,7 @@
 
     def back(g):
         take(3, g)
+        sent(1, g)
         strike_cells_dft(1.0, u2.at[g], strike_tw_ref, strike_table_ref, w1.at[g], held_part)
         go(4, g)
 
@@ -545,6 +544,14 @@
         @pl.when(thin)
         def _():
             swap.wait_send()
+            if zone < modes:
+
+                @pl.loop(0, count)
+                def _(g):
+                    t2[g, :, :, pl.ds(zone, modes - zone), :] = jnp.zeros(
+                        (*t2.shape[1:3], modes - zone, narrow), F32
+                    )
+
             row = lax.broadcasted_iota(jnp.int32, now_ref.shape, 0)
             weight[...] = jnp.where(lax.rem(row, modes) == 0, scale * now_ref[...], 0.0)
 
@@ -700,10 +707,10 @@
                     col_in[1, rows, k : k + 1],
                 )
                 if z + 1 < layers:
-                    total = total + 0.5 * stress_held[slot, sz, z + 1, 8 : size + 8, :]
+                    total = total + stress_held[slot, sz, z + 1, 8 : size + 8, :]
                 if z > 0:
-                    total = total - 0.5 * stress_held[slot, sz, z - 1, 8 : size + 8, :]
-                value = v_held[component, z, rows, :] + COURANT * total
+                    total = total - stress_held[slot, sz, z - 1, 8 : size + 8, :]
+                value = v_held[component, z, rows, :] + (0.5 * COURANT) * total
                 v_held[component, z, rows, :] = value
                 if z > 0:
                     col_new[0, rows, k : k + 1] = value[:, 0:1]
@@ -719,8 +726,6 @@
     go(0, 1)
     for load in edge_loads:
         load.start()
-    for c in stress_rows:
-        c.start()
     velocity_load.start()
     for load in tile_loads(0):
         load.start()
@@ -785,6 +790,11 @@
         def _():
             across(s - 1)
 
+        @pl.when(s == 1)
+        def _():
+            for c in stress_rows:
+                c.start()
+
         turned = s - first_back - (s > gap).astype(jnp.int32)
 
         @pl.when(jnp.logical_and(jnp.logical_and(turned >= 0, turned < count), s != gap))
@@ -808,7 +818,6 @@
     @pl.loop(0, count)
     def _(g):
         take(5, g)
-        spread_end(g)
         c = lax.div(g, parts)
         lanes = pl.ds(pl.multiple_of(lax.rem(g, parts) * narrow, narrow), narrow)
         high = cells // sizes["bx"]
@@ -839,6 +848,13 @@
     top_store.wait()
     for c in stress_rows + stress_cols + new_cols + deep_rows + top_cols:
         c.wait_send()
+
+    @pl.loop(0, count)
+    def _(g):
+        spread_end(g)
+        for stage in (0, 3, 4, 5):
+            sent(stage, g)
+
     for c in top_rows:
         c.wait()
 

time: 181 us -> 184 us (1.017)
  Pallas kernels: 181 us -> 183 us
    pallas_call x1, Pallas kernels: 163 us -> 165 us  [fault_velocity(): pl.pallas_call(partial(fault_kernel, scale), out_shape=[struct(velocity.s...]
where the time goes in v3:
time: 184 us
  Pallas kernels  183 us (99%)
    pallas_call x1, Pallas kernels, fault_velocity(): pl.pallas_call(partial(fault_kernel, scale), out_shape=[struct(velocity.s...  165 us
    pallas_call x1, Pallas kernels, local(): pl.pallas_call(stress_step, grid=(cells // tile,), in_specs=[tile_spec(ve...  17.6 us

profile of v3, /device:TPU:0, one launch (start us, length us, event | category | flops | bytes accessed | tf_op | source)
XLA Modules:
  0.0 183.7 jit_solution(6476669982840154377)
XLA Ops:
  0.6 165.4 %fault_velocity.1 = (f32[3,4,256,512]{3,2,1,0:T(8,128)}, f32[2,3,4,8,512]{4,3,2,1,0:T(8,128)}, f32[2,256,128]{2,1,0:T(8,128)}) custom-call(f32[3,8,32,512]{3,2,1,0:T(8,128)} %bitcast.1, f32[8,8,256]{2,1,0:T(8,128)} %constant.11.clone.turns_ref, bf16[2,2,256,256]{3,2,1,0:T(8,128)(2,1)} %constant.10.clone.strike_table_ref, ...), custom_call_target="tpu_custom_call" | custom-call | tf_op jit(solution)/shard_map/fault_velocity/pallas_call | solution.py:877
  166.0 17.6 %stress_step.1 = (f32[3,4,256,512]{3,2,1,0:T(8,128)}, f32[6,4,256,512]{3,2,1,0:T(8,128)}) custom-call(f32[3,4,256,512]{3,2,1,0:T(8,128)} %get-tuple-element.5.v_ref.prev_ref.next_ref, f32[3,4,256,512]{3,2,1,0:T(8,128)} %get-tuple-element.5.v_ref.prev_ref.next_ref, f32[3,4,256,512]{3,2,1,0:T(8,128)} %get-tuple-element.5.v_ref.prev_ref.next_ref, ...), custom_call_target="tpu_custom_call" | custom-call | flops 20000000 | bytes 31457280 | tf_op jit(solution)/shard_map/stress_step/pallas_call | solution.py:956

commit v4 on v2

--- a/solution.py
+++ b/solution.py
@@ -231,9 +231,9 @@
     scale,
     face_ref,
     turns_ref,
-    strike_table_ref,
+    strike_source,
     dip_tw_ref,
-    dip_table_ref,
+    dip_source,
     kernel_ref,
     history_ref,
     velocity_ref,
@@ -253,6 +253,8 @@
     held_part,
     weight,
     strike_tw_ref,
+    strike_table_ref,
+    dip_table_ref,
     lags,
     lag_held,
     past_ref,
@@ -298,12 +300,6 @@
     forward = jnp.logical_or(full, strike == 0)
     mirror = (lax.rem(sizes["bx"] - strike, sizes["bx"]), sizes["by"] - 1 - dip)
 
-    @pl.when(thin)
-    def _():
-        @pl.loop(0, count)
-        def _(g):
-            t2[g] = jnp.zeros(t2.shape[1:], F32)
-
     layers, cells, width = v_held.shape[1:]
     components = past_ref.shape[0]
     lag_loads = [
@@ -324,7 +320,13 @@
             for l in range(sizes["by"])
         ]
 
-    for load in lag_loads:
+    table_loads = [
+        pltpu.make_async_copy(source, landing, lag_sem.at[sizes["by"] + i])
+        for i, (source, landing) in enumerate(
+            ((strike_source, strike_table_ref), (dip_source, dip_table_ref))
+        )
+    ]
+    for load in lag_loads + table_loads:
         load.start()
     barrier = pltpu.get_barrier_semaphore()
     pl.semaphore_signal(barrier, 1, device_id=mirror, device_id_type=pl.DeviceIdType.MESH)
@@ -545,6 +547,14 @@
         @pl.when(thin)
         def _():
             swap.wait_send()
+            if zone < modes:
+
+                @pl.loop(0, count)
+                def _(g):
+                    t2[g, :, :, pl.ds(zone, modes - zone), :] = jnp.zeros(
+                        (*t2.shape[1:3], modes - zone, narrow), F32
+                    )
+
             row = lax.broadcasted_iota(jnp.int32, now_ref.shape, 0)
             weight[...] = jnp.where(lax.rem(row, modes) == 0, scale * now_ref[...], 0.0)
 
@@ -762,7 +772,7 @@
 
         @pl.when(s == 0)
         def _():
-            for load in lag_loads:
+            for load in lag_loads + table_loads:
                 load.wait()
 
         @pl.when(jnp.logical_and(s == 0, jnp.logical_not(full)))
@@ -865,7 +875,7 @@
             struct((2, count, layers, 8, width)),
             struct((2, cells, block)),
         ],
-        in_specs=[anywhere] + [vmem] * len(tables) + [anywhere] * 4,
+        in_specs=[anywhere, vmem, anywhere, vmem] + [anywhere] * 5,
         out_specs=[anywhere, vmem, vmem],
         scratch_shapes=[
             *[pltpu.VMEM(s, F32) for s in (flat, wide, wide, tall, tall, tall, tall, wide)],
@@ -873,10 +883,12 @@
             pltpu.VMEM((2, cells, narrow), F32),
             pltpu.VMEM((cells, width), F32),
             pltpu.VMEM((cells, block), F32),
+            pltpu.VMEM(tables[1].shape, BF16),
+            pltpu.VMEM(tables[3].shape, BF16),
             pltpu.VMEM((kernel.shape[0], cells, width), F32),
             pltpu.VMEM((2, history.shape[0], cells, width), F32),
             pltpu.VMEM((count, 2, cells, width), F32),
-            pltpu.SemaphoreType.DMA((dip_count,)),
+            pltpu.SemaphoreType.DMA((dip_count + 2,)),
             pltpu.SemaphoreType.DMA((2, dip_count)),
             pltpu.SemaphoreType.DMA((7, chunks)),
             pltpu.SemaphoreType.DMA((6, chunks)),

time: 181 us -> 181 us (level)
  no operation moved by 1% of the time
where the time goes in v4:
time: 181 us
  Pallas kernels  180 us (99%)
    pallas_call x1, Pallas kernels, fault_velocity(): pl.pallas_call(partial(fault_kernel, scale), out_shape=[struct(velocity.s...  162 us
    pallas_call x1, Pallas kernels, local(): pl.pallas_call(stress_step, grid=(cells // tile,), in_specs=[tile_spec(ve...  17.8 us

profile of v4, /device:TPU:0, one launch (start us, length us, event | category | flops | bytes accessed | tf_op | source)
XLA Modules:
  0.0 180.6 jit_solution(8130685694090248948)
XLA Ops:
  0.6 162.1 %fault_velocity.1 = (f32[3,4,256,512]{3,2,1,0:T(8,128)}, f32[2,3,4,8,512]{4,3,2,1,0:T(8,128)}, f32[2,256,128]{2,1,0:T(8,128)}) custom-call(f32[3,8,32,512]{3,2,1,0:T(8,128)} %bitcast.1, f32[8,8,256]{2,1,0:T(8,128)} %constant.11.clone.turns_ref, bf16[2,2,256,256]{3,2,1,0:T(8,128)(2,1)} %constant.10.clone.strike_source, ...), custom_call_target="tpu_custom_call" | custom-call | tf_op jit(solution)/shard_map/fault_velocity/pallas_call | solution.py:871
  162.7 17.8 %stress_step.1 = (f32[3,4,256,512]{3,2,1,0:T(8,128)}, f32[6,4,256,512]{3,2,1,0:T(8,128)}) custom-call(f32[3,4,256,512]{3,2,1,0:T(8,128)} %get-tuple-element.5.v_ref.prev_ref.next_ref, f32[3,4,256,512]{3,2,1,0:T(8,128)} %get-tuple-element.5.v_ref.prev_ref.next_ref, f32[3,4,256,512]{3,2,1,0:T(8,128)} %get-tuple-element.5.v_ref.prev_ref.next_ref, ...), custom_call_target="tpu_custom_call" | custom-call | flops 20000000 | bytes 31457280 | tf_op jit(solution)/shard_map/stress_step/pallas_call | solution.py:952
